TPU v7x, 32 devices: a whole 2x2x4 slice. The times are simulated.
32 devices in a mesh: fsdp: 16 (over z, x, core), grp: 2 (over y).
Axes of the slice: x: 2, y: 2, z: 4, core: 2. Of those that a mesh axis runs over, the one named last changes fastest.
Arguments:
- block_in: bfloat16 [32, 680, 1024], P(('fsdp', 'grp')), may hold values from -6 to 6
- cotangent: bfloat16 [32, 680, 1024], P(('fsdp', 'grp')), may hold values from -6 to 6
- stop_scale: int32 [32], P(('fsdp', 'grp')), may hold values from 6 to 10
- class_label: int32 [32], P(('fsdp', 'grp')), may hold values from 0 to 999
- w_qkv: float32 [1024, 3072], P(('fsdp', 'grp')), may hold values from -0.1875 to 0.1875
- w_proj: float32 [1024, 1024], P(('fsdp', 'grp')), may hold values from -0.75 to 0.75
- w_fc1: float32 [1024, 4096], P(('fsdp', 'grp')), may hold values from -0.1875 to 0.1875
- w_fc2: float32 [4096, 1024], P(('fsdp', 'grp')), may hold values from -0.09375 to 0.09375
- w_ada: float32 [1024, 6144], P(('fsdp', 'grp')), may hold values from -0.1875 to 0.1875
- w_table: float32 [1000, 1024], P(None, ('fsdp', 'grp')), may hold values from -6 to 6
- m_qkv: float32 [1024, 3072], P(('fsdp', 'grp')), may hold values from -320 to 320
- m_proj: float32 [1024, 1024], P(('fsdp', 'grp')), may hold values from -96 to 96
- m_fc1: float32 [1024, 4096], P(('fsdp', 'grp')), may hold values from -256 to 256
- m_fc2: float32 [4096, 1024], P(('fsdp', 'grp')), may hold values from -256 to 256
- m_ada: float32 [1024, 6144], P(('fsdp', 'grp')), may hold values from -384 to 384
- m_table: float32 [1000, 1024], P(None, ('fsdp', 'grp')), may hold values from -80 to 80
- v_qkv: float32 [1024, 3072], P(('fsdp', 'grp')), may hold values from 2720 to 10880
- v_proj: float32 [1024, 1024], P(('fsdp', 'grp')), may hold values from 244.8 to 979.2
- v_fc1: float32 [1024, 4096], P(('fsdp', 'grp')), may hold values from 1740.8 to 6963.2
- v_fc2: float32 [4096, 1024], P(('fsdp', 'grp')), may hold values from 1740.8 to 6963.2
- v_ada: float32 [1024, 6144], P(('fsdp', 'grp')), may hold values from 3916.8 to 15667.2
- v_table: float32 [1000, 1024], P(None, ('fsdp', 'grp')), may hold values from 170 to 680
Outputs:
- block_out: bfloat16 [32, 680, 1024], P(('fsdp', 'grp'))
- grad_in: float32 [32, 680, 1024], P(('fsdp', 'grp'))
- new_qkv: float32 [1024, 3072], P(('fsdp', 'grp'))
- new_proj: float32 [1024, 1024], P(('fsdp', 'grp'))
- new_fc1: float32 [1024, 4096], P(('fsdp', 'grp'))
- new_fc2: float32 [4096, 1024], P(('fsdp', 'grp'))
- new_ada: float32 [1024, 6144], P(('fsdp', 'grp'))
- new_table: float32 [1000, 1024], P(None, ('fsdp', 'grp'))
- half_qkv: bfloat16 [1024, 3072], P(('fsdp', 'grp'))
- half_proj: bfloat16 [1024, 1024], P(('fsdp', 'grp'))
- half_fc1: bfloat16 [1024, 4096], P(('fsdp', 'grp'))
- half_fc2: bfloat16 [4096, 1024], P(('fsdp', 'grp'))
- half_ada: bfloat16 [1024, 6144], P(('fsdp', 'grp'))
- half_table: bfloat16 [1000, 1024], P(None, ('fsdp', 'grp'))
- first_qkv: float32 [1024, 3072], P(('fsdp', 'grp'))
- first_proj: float32 [1024, 1024], P(('fsdp', 'grp'))
- first_fc1: float32 [1024, 4096], P(('fsdp', 'grp'))
- first_fc2: float32 [4096, 1024], P(('fsdp', 'grp'))
- first_ada: float32 [1024, 6144], P(('fsdp', 'grp'))
- first_table: float32 [1000, 1024], P(None, ('fsdp', 'grp'))
- second_qkv: float32 [1024, 3072], P(('fsdp', 'grp'))
- second_proj: float32 [1024, 1024], P(('fsdp', 'grp'))
- second_fc1: float32 [1024, 4096], P(('fsdp', 'grp'))
- second_fc2: float32 [4096, 1024], P(('fsdp', 'grp'))
- second_ada: float32 [1024, 6144], P(('fsdp', 'grp'))
- second_table: float32 [1000, 1024], P(None, ('fsdp', 'grp'))
Inputs may be any that keep to these rules, and one draw needn't show every extreme that they name: An item holds the tokens of its first stop_scale scales, from the start of its 680 slots; later slots are padding.
All inputs are finite; a program needn't handle non-finite values.
Results may differ from a plain program's by a relative error of at most 0.017.
The roundings to bfloat16 on the way count: a program that leaves them out, or rounds other values in their place, can miss the bound.
Values may be sent and summed in bfloat16 or wider, within the bound.
No kernel may reach another device: no remote copies, remote signals or barrier semaphores. Data moves between devices by JAX's collectives and lax.ppermute only.
A program may use at most 256 MiB of HBM per device.

v0:
```python
import jax
import jax.numpy as jnp
import numpy as np
from jax import lax
from jax.sharding import PartitionSpec as P

D = 1024
HEADS = 16
HEAD = 64
FF = 4096
SCALES = 10
STEP = 3


patch_sides = (1, 2, 3, 4, 5, 6, 8, 10, 13, 16)
norm_eps = 1e-06
adam_eps = 1e-08
decay = 0.05
highest = lax.Precision.HIGHEST


def scale_layout(slots):
    squares = np.array(patch_sides[:SCALES], dtype=np.int64) ** 2
    bounds = np.cumsum(squares)
    scale_ids = np.searchsorted(bounds, np.arange(slots), side="right")
    return (bounds.astype(np.int32), scale_ids.astype(np.int32))


def norm_rows(values):
    centre = values - jnp.mean(values, axis=-1, keepdims=True)
    spread = jnp.mean(centre * centre, axis=-1, keepdims=True)
    return centre * lax.rsqrt(spread + norm_eps)


def modulate(values, scale_row, shift_row):
    return norm_rows(values) * (1.0 + scale_row) + shift_row


def gelu_tanh(values):
    return jax.nn.gelu(values, approximate=True)


def learn_rates():
    return (D ** (-0.5), (D // 16) ** (-0.5), D ** (-0.5), FF ** (-0.5), D ** (-0.5), 1.0)


def adamw(weight, gradient, first, second, bias_one, bias_two, rate):
    first_new = 0.5 * first + 0.5 * gradient
    second_new = 0.5 * second + 0.5 * gradient * gradient
    update = first_new / bias_one / (jnp.sqrt(second_new / bias_two) + adam_eps) + decay * weight
    weight_new = weight - rate * update
    return (weight_new, weight_new.astype(jnp.bfloat16), first_new, second_new)


def contract_rows(former, latter):
    return lax.dot_general(
        former, latter, (((0,), (0,)), ((), ())), preferred_element_type=jnp.float32
    )


def contract_cols(former, latter):
    return lax.dot_general(
        former, latter, (((1,), (1,)), ((), ())), preferred_element_type=jnp.float32
    )


def masked_scores(queries, key_rows, allow):
    raw = jnp.einsum("qhd,khd->hqk", queries, key_rows, preferred_element_type=jnp.float32) * 0.125
    return jnp.where(allow[None], raw, -1e30)


def attend_forward(inputs):
    queries, key_rows, values, allow = inputs
    scores = masked_scores(queries, key_rows, allow)
    largest = jnp.max(scores, axis=-1, keepdims=True)
    expo = jnp.exp(scores - largest)
    totals = jnp.sum(expo, axis=-1, keepdims=True)
    probs_low = (expo / totals).astype(jnp.bfloat16)
    log_total = largest + jnp.log(totals)
    context = jnp.einsum("hqk,khd->qhd", probs_low, values, preferred_element_type=jnp.float32)
    return (context.astype(jnp.bfloat16), log_total)


def attend_backward(inputs):
    queries, key_rows, values, allow, log_total, d_context = inputs
    probs = jnp.exp(masked_scores(queries, key_rows, allow) - log_total)
    probs_low = probs.astype(jnp.bfloat16)
    d_values = jnp.einsum("hqk,qhd->khd", probs_low, d_context, preferred_element_type=jnp.float32)
    d_probs = jnp.einsum("qhd,khd->hqk", d_context, values, preferred_element_type=jnp.float32)
    inner_sum = jnp.sum(probs * d_probs, axis=-1, keepdims=True)
    d_scores = (probs * (d_probs - inner_sum)).astype(jnp.bfloat16)
    d_queries = (
        jnp.einsum("hqk,khd->qhd", d_scores, key_rows, preferred_element_type=jnp.float32) * 0.125
    )
    d_keys = (
        jnp.einsum("hqk,qhd->khd", d_scores, queries, preferred_element_type=jnp.float32) * 0.125
    )
    return jnp.stack([d_queries, d_keys, d_values], axis=1).astype(jnp.bfloat16)


def per_device(
    block_in,
    cotangent,
    stop_scale,
    class_label,
    w_qkv,
    w_proj,
    w_fc1,
    w_fc2,
    w_ada,
    w_table,
    m_qkv,
    m_proj,
    m_fc1,
    m_fc2,
    m_ada,
    m_table,
    v_qkv,
    v_proj,
    v_fc1,
    v_fc2,
    v_ada,
    v_table,
):
    items, slots, width = block_in.shape
    row_count = items * slots
    bounds, scale_ids = scale_layout(slots)
    picked = jnp.arange(SCALES)[None, :] == stop_scale[:, None] - 1
    lengths = jnp.sum(jnp.where(picked, jnp.asarray(bounds)[None, :], 0), axis=1)
    position = jnp.arange(slots)
    valid = (position[None, :] < lengths[:, None]).astype(jnp.float32)
    scale_table = jnp.asarray(scale_ids)
    allowed = (scale_table[None, None, :] <= scale_table[None, :, None]) & (
        position[None, None, :] < lengths[:, None, None]
    )
    cast_qkv = w_qkv.astype(jnp.bfloat16)
    cast_proj = w_proj.astype(jnp.bfloat16)
    cast_fc1 = w_fc1.astype(jnp.bfloat16)
    cast_fc2 = w_fc2.astype(jnp.bfloat16)
    cast_ada = w_ada.astype(jnp.bfloat16)
    cast_table = w_table.astype(jnp.bfloat16)
    wide_ada, wide_table = (
        lax.all_gather(cast_ada, ("fsdp", "grp"), axis=0, tiled=True),
        lax.all_gather(cast_table, ("fsdp", "grp"), axis=1, tiled=True),
    )
    onehot = (class_label[:, None] == jnp.arange(wide_table.shape[0])[None, :]).astype(jnp.bfloat16)
    cond = jnp.dot(onehot, wide_table, preferred_element_type=jnp.float32)
    silu_out, silu_back = jax.vjp(jax.nn.silu, cond)
    lifted_low = silu_out.astype(jnp.bfloat16)
    ada = jnp.dot(lifted_low, wide_ada, preferred_element_type=jnp.float32)
    pieces = [ada[:, offset * width : (offset + 1) * width][:, None, :] for offset in range(6)]
    gamma_one, scale_one, shift_one, gamma_two, scale_two, shift_two = pieces
    tokens = block_in.astype(jnp.float32)
    wide_qkv, wide_proj = (
        lax.all_gather(cast_qkv, ("fsdp", "grp"), axis=0, tiled=True),
        lax.all_gather(cast_proj, ("fsdp", "grp"), axis=0, tiled=True),
    )
    hidden, modulate_one = jax.vjp(modulate, tokens, scale_one, shift_one)
    hidden_low = hidden.astype(jnp.bfloat16).reshape(row_count, width)
    packed = jnp.dot(hidden_low, wide_qkv, preferred_element_type=jnp.float32)
    packed = packed.astype(jnp.bfloat16).reshape(items, slots, 3, HEADS, HEAD)
    queries = packed[:, :, 0]
    key_rows = packed[:, :, 1]
    values = packed[:, :, 2]
    context, log_total = lax.map(attend_forward, (queries, key_rows, values, allowed))
    context = context.reshape(row_count, width)
    attended = jnp.dot(context, wide_proj, preferred_element_type=jnp.float32).reshape(
        items, slots, width
    )
    middle = tokens + gamma_one * attended
    wide_fc1, wide_fc2 = (
        lax.all_gather(cast_fc1, ("fsdp", "grp"), axis=0, tiled=True),
        lax.all_gather(cast_fc2, ("fsdp", "grp"), axis=0, tiled=True),
    )
    second, modulate_two = jax.vjp(modulate, middle, scale_two, shift_two)
    second_low = second.astype(jnp.bfloat16).reshape(row_count, width)
    inner = jnp.dot(second_low, wide_fc1, preferred_element_type=jnp.float32)
    activated, gelu_back = jax.vjp(gelu_tanh, inner)
    activated_low = activated.astype(jnp.bfloat16)
    branch = jnp.dot(activated_low, wide_fc2, preferred_element_type=jnp.float32).reshape(
        items, slots, width
    )
    block_out = ((middle + gamma_two * branch) * valid[:, :, None]).astype(jnp.bfloat16)
    upstream = cotangent.astype(jnp.float32) * valid[:, :, None]
    d_gamma_two = jnp.sum(upstream * branch, axis=1)
    d_branch = (upstream * gamma_two).astype(jnp.bfloat16).reshape(row_count, width)
    grad_fc2 = contract_rows(activated_low, d_branch)
    (d_inner,) = gelu_back(contract_cols(d_branch, wide_fc2))
    d_inner_low = d_inner.astype(jnp.bfloat16)
    grad_fc1 = contract_rows(second_low, d_inner_low)
    sum_fc1, sum_fc2 = (
        lax.psum_scatter(grad_fc1, ("fsdp", "grp"), scatter_dimension=0, tiled=True),
        lax.psum_scatter(grad_fc2, ("fsdp", "grp"), scatter_dimension=0, tiled=True),
    )
    d_second = contract_cols(d_inner_low, wide_fc1).reshape(items, slots, width)
    d_middle_part, d_scale_two, d_shift_two = modulate_two(d_second)
    d_middle = upstream + d_middle_part
    d_gamma_one = jnp.sum(d_middle * attended, axis=1)
    d_attended = (d_middle * gamma_one).astype(jnp.bfloat16).reshape(row_count, width)
    grad_proj = contract_rows(context, d_attended)
    d_context = (
        contract_cols(d_attended, wide_proj).astype(jnp.bfloat16).reshape(items, slots, HEADS, HEAD)
    )
    d_packed = lax.map(attend_backward, (queries, key_rows, values, allowed, log_total, d_context))
    d_packed = d_packed.reshape(row_count, 3 * width)
    grad_qkv = contract_rows(hidden_low, d_packed)
    sum_qkv, sum_proj = (
        lax.psum_scatter(grad_qkv, ("fsdp", "grp"), scatter_dimension=0, tiled=True),
        lax.psum_scatter(grad_proj, ("fsdp", "grp"), scatter_dimension=0, tiled=True),
    )
    d_hidden = contract_cols(d_packed, wide_qkv).reshape(items, slots, width)
    d_tokens, d_scale_one, d_shift_one = modulate_one(d_hidden)
    grad_in = d_middle + d_tokens
    d_ada = jnp.concatenate(
        [
            d_gamma_one,
            d_scale_one[:, 0],
            d_shift_one[:, 0],
            d_gamma_two,
            d_scale_two[:, 0],
            d_shift_two[:, 0],
        ],
        axis=1,
    ).astype(jnp.bfloat16)
    grad_ada = contract_rows(lifted_low, d_ada)
    (d_cond,) = silu_back(contract_cols(d_ada, wide_ada))
    grad_table = lax.dot_general(
        onehot.astype(jnp.float32), d_cond, (((0,), (0,)), ((), ())), precision=highest
    )
    sum_ada, sum_table = (
        lax.psum_scatter(grad_ada, ("fsdp", "grp"), scatter_dimension=0, tiled=True),
        lax.psum_scatter(grad_table, ("fsdp", "grp"), scatter_dimension=1, tiled=True),
    )
    counter = jnp.float32(STEP)
    bias_one = 1.0 - jnp.power(jnp.float32(0.5), counter)
    bias_two = 1.0 - jnp.power(jnp.float32(0.5), counter)
    rates = learn_rates()
    upd_qkv = adamw(w_qkv, sum_qkv, m_qkv, v_qkv, bias_one, bias_two, rates[0])
    upd_proj = adamw(w_proj, sum_proj, m_proj, v_proj, bias_one, bias_two, rates[1])
    upd_fc1 = adamw(w_fc1, sum_fc1, m_fc1, v_fc1, bias_one, bias_two, rates[2])
    upd_fc2 = adamw(w_fc2, sum_fc2, m_fc2, v_fc2, bias_one, bias_two, rates[3])
    upd_ada = adamw(w_ada, sum_ada, m_ada, v_ada, bias_one, bias_two, rates[4])
    upd_table = adamw(w_table, sum_table, m_table, v_table, bias_one, bias_two, rates[5])
    return (
        block_out,
        grad_in,
        upd_qkv[0],
        upd_proj[0],
        upd_fc1[0],
        upd_fc2[0],
        upd_ada[0],
        upd_table[0],
        upd_qkv[1],
        upd_proj[1],
        upd_fc1[1],
        upd_fc2[1],
        upd_ada[1],
        upd_table[1],
        upd_qkv[2],
        upd_proj[2],
        upd_fc1[2],
        upd_fc2[2],
        upd_ada[2],
        upd_table[2],
        upd_qkv[3],
        upd_proj[3],
        upd_fc1[3],
        upd_fc2[3],
        upd_ada[3],
        upd_table[3],
    )


def solution(mesh):
    return jax.shard_map(
        per_device,
        mesh=mesh,
        in_specs=(
            P(("fsdp", "grp"), None, None),
            P(("fsdp", "grp"), None, None),
            P(("fsdp", "grp")),
            P(("fsdp", "grp")),
            P(("fsdp", "grp"), None),
            P(("fsdp", "grp"), None),
            P(("fsdp", "grp"), None),
            P(("fsdp", "grp"), None),
            P(("fsdp", "grp"), None),
            P(None, ("fsdp", "grp")),
            P(("fsdp", "grp"), None),
            P(("fsdp", "grp"), None),
            P(("fsdp", "grp"), None),
            P(("fsdp", "grp"), None),
            P(("fsdp", "grp"), None),
            P(None, ("fsdp", "grp")),
            P(("fsdp", "grp"), None),
            P(("fsdp", "grp"), None),
            P(("fsdp", "grp"), None),
            P(("fsdp", "grp"), None),
            P(("fsdp", "grp"), None),
            P(None, ("fsdp", "grp")),
        ),
        out_specs=(
            P(("fsdp", "grp"), None, None),
            P(("fsdp", "grp"), None, None),
            P(("fsdp", "grp"), None),
            P(("fsdp", "grp"), None),
            P(("fsdp", "grp"), None),
            P(("fsdp", "grp"), None),
            P(("fsdp", "grp"), None),
            P(None, ("fsdp", "grp")),
            P(("fsdp", "grp"), None),
            P(("fsdp", "grp"), None),
            P(("fsdp", "grp"), None),
            P(("fsdp", "grp"), None),
            P(("fsdp", "grp"), None),
            P(None, ("fsdp", "grp")),
            P(("fsdp", "grp"), None),
            P(("fsdp", "grp"), None),
            P(("fsdp", "grp"), None),
            P(("fsdp", "grp"), None),
            P(("fsdp", "grp"), None),
            P(None, ("fsdp", "grp")),
            P(("fsdp", "grp"), None),
            P(("fsdp", "grp"), None),
            P(("fsdp", "grp"), None),
            P(("fsdp", "grp"), None),
            P(("fsdp", "grp"), None),
            P(None, ("fsdp", "grp")),
        ),
        check_vma=False,
    )
```

profile of v0, /device:TPU:0, one launch (start us, length us, event | category | flops | bytes accessed | tf_op | source)
XLA Modules:
  0.0 2082.5 jit_solution(14357250446636522632)
XLA Ops:
  7.3 1.7 convert_element_type.124
  9.0 1.9 convert_element_type.126
  11.0 1.7 convert_element_type.128
  12.8 1.5 convert_element_type.133
  14.4 0.7 convert_element_type.135
  16.6 0.6 fusion.58
  17.2 0.6 iota_compare_fusion
  17.9 0.7 fusion.60
  20.3 50.7 %all-gather.7.cloned.1.call-done = bf16[1000,1024]{0,1:T(8,128)(2,1)} async-done(((bf16[1000,32]{0,1:T(8,128)(2,1)}), bf16[1000,1024]{0,1:T(8,128)(2,1)}) %all-gather.7.cloned.1.call-update) | async-done | bytes 2048016 | tf_op jit(solution)/shard_map/all_gather | solution.py:144
  71.0 2.2 fusion.87
  73.2 0.6 fusion.82
  73.8 95.5 %all-gather.9.cloned.1.call-done = bf16[1024,6144]{1,0:T(8,128)(2,1)} async-done(((bf16[32,6144]{1,0:T(8,128)(2,1)}), bf16[1024,6144]{1,0:T(8,128)(2,1)}) %all-gather.9.cloned.1.call-update) | async-done | bytes 12582928 | tf_op jit(solution)/shard_map/all_gather | solution.py:143
  169.3 6.3 fusion.88
  175.7 64.9 %all-gather.11.cloned.1.call-done = bf16[1024,3072]{1,0:T(8,128)(2,1)} async-done(((bf16[32,3072]{1,0:T(8,128)(2,1)}), bf16[1024,3072]{1,0:T(8,128)(2,1)}) %all-gather.11.cloned.1.call-update) | async-done | bytes 6291472 | tf_op jit(solution)/shard_map/all_gather | solution.py:155
  240.6 9.9 convolution_convert_fusion
  250.5 6.5 copy.59
  256.9 15.8 fusion.86
  272.8 13.5 fusion
  286.3 15.6 fusion.33
  301.9 5.8 fusion.84
  308.1 70.9 %all-gather.15.cloned.1.call-done = bf16[1024,4096]{1,0:T(8,128)(2,1)} async-done(((bf16[32,4096]{1,0:T(8,128)(2,1)}), bf16[1024,4096]{1,0:T(8,128)(2,1)}) %all-gather.15.cloned.1.call-update) | async-done | bytes 8388624 | tf_op jit(solution)/shard_map/all_gather | solution.py:172
  379.0 9.1 fusion.67
  388.1 4.0 copy-done.42
  392.2 11.7 fusion.45
  404.0 356.0 %reduce-scatter.13.cloned.1.call-done = f32[128,1024]{1,0:T(8,128)} async-done(((f32[4096,1024]{1,0:T(8,128)}), f32[128,1024]{1,0:T(8,128)}) %reduce-scatter.13.cloned.1.call-update) | async-done | bytes 524304 | tf_op jit(solution)/shard_map/reduce_scatter | solution.py:193
  760.0 3.0 fusion.74
  763.7 78.6 %all-gather.17.cloned.1.call-done = bf16[4096,1024]{1,0:T(8,128)(2,1)} async-done(((bf16[128,1024]{1,0:T(8,128)(2,1)}), bf16[4096,1024]{1,0:T(8,128)(2,1)}) %all-gather.17.cloned.1.call-update) | async-done | bytes 8388624 | tf_op jit(solution)/shard_map/all_gather | solution.py:173
  842.2 16.6 fusion.12
  858.9 10.9 fusion.24
  869.9 0.8 fusion.83
  870.7 0.6 copy-done.3
  871.3 1.5 copy-done.8
  872.9 1.0 copy-done.40
  873.8 3.1 convolution_convert_fusion.1
  876.9 2.6 copy.61
  879.4 15.5 fusion.30
  895.0 26.3 %multiply_reduce_fusion = (f32[16,680]{1,0:T(8,128)S(1)}, f32[16,680,680]{1,2,0:T(8,128)}) fusion(f32[16,680,680]{1,2,0:T(8,128)} %get-tuple-element.117, f32[16,680]{1,0:T(8,128)S(1)} %log_add_fusion, bf16[680,16,64]{0,2,1:T(8,128)(2,1)} %bitcast.135, bf16[1,680,3,16,64]{1,4,3,2,0:T(8,128)(2,1)} %bitcast.131), kind=kOutput, calls=%fused_computation.1 | convolution fusion | flops 969179520 | bytes 66249728 | tf_op jit(solution)/shard_map/while/body/eval_jaxpr/qhd,khd->hqk/dot_general | solution.py:89
  921.2 27.6 %multiply_convert_fusion = bf16[16,680,680]{1,2,0:T(8,128)(2,1)} fusion(f32[16,680,680]{1,2,0:T(8,128)} %get-tuple-element.121, f32[16,680,680]{1,2,0:T(8,128)} %get-tuple-element.117, f32[16,680]{1,0:T(8,128)S(1)} %get-tuple-element.120, f32[16,680]{1,0:T(8,128)S(1)} %log_add_fusion), kind=kLoop, calls=%fused_computation | loop fusion | flops 29593600 | bytes 74071040 | tf_op jit(solution)/shard_map/while/body/eval_jaxpr/convert_element_type | solution.py:91
  948.9 12.4 multiply_bitcast_fusion
  961.3 10.5 multiply_bitcast_fusion.1
  971.7 2.0 reduce_sum.187
  973.7 2.9 maximum_convert_fusion
  976.7 11.2 fusion.23
  987.9 2.0 reduce_sum.184
  990.0 3.6 fusion.21
  993.6 16.2 fusion.25
  1009.9 7.9 fusion.89
  1017.9 2.3 broadcast_multiply_fusion.1
  1020.3 6.7 fusion.40
  1027.1 0.6 copy-done.37
  1027.7 11.1 fusion.61
  1038.9 0.6 copy-done.18
  1039.5 13.2 fusion.65
  1053.3 11.6 broadcast_multiply_fusion
  1065.0 95.4 %reduce-scatter.17.cloned.1.call-done = f32[1000,32]{0,1:T(8,128)} async-done(((f32[1000,1024]{0,1:T(8,128)}), f32[1000,32]{0,1:T(8,128)}) %reduce-scatter.17.cloned.1.call-update) | async-done | bytes 128016 | tf_op jit(solution)/shard_map/reduce_scatter | solution.py:232
  1160.4 1.7 fusion.70
  1162.2 139.2 %reduce-scatter.9.cloned.1.call-done = f32[32,1024]{1,0:T(8,128)} async-done(((f32[1024,1024]{1,0:T(8,128)}), f32[32,1024]{1,0:T(8,128)}) %reduce-scatter.9.cloned.1.call-update) | async-done | bytes 131088 | tf_op jit(solution)/shard_map/reduce_scatter | solution.py:209
  1301.4 1.7 fusion.78
  1303.1 156.4 %reduce-scatter.7.cloned.1.call-done = f32[32,3072]{1,0:T(8,128)} async-done(((f32[1024,3072]{1,0:T(8,128)}), f32[32,3072]{1,0:T(8,128)}) %reduce-scatter.7.cloned.1.call-update) | async-done | bytes 393232 | tf_op jit(solution)/shard_map/reduce_scatter | solution.py:208
  1459.5 2.5 fusion.80
  1462.0 356.4 %reduce-scatter.11.cloned.1.call-done = f32[32,4096]{1,0:T(8,128)} async-done(((f32[1024,4096]{1,0:T(8,128)}), f32[32,4096]{1,0:T(8,128)}) %reduce-scatter.11.cloned.1.call-update) | async-done | bytes 524304 | tf_op jit(solution)/shard_map/reduce_scatter | solution.py:192
  1818.4 2.9 fusion.76
  1821.2 251.1 %reduce-scatter.15.cloned.1.call-done = f32[32,6144]{1,0:T(8,128)} async-done(((f32[1024,6144]{1,0:T(8,128)}), f32[32,6144]{1,0:T(8,128)}) %reduce-scatter.15.cloned.1.call-update) | async-done | bytes 786448 | tf_op jit(solution)/shard_map/reduce_scatter | solution.py:231
  2072.4 3.1 fusion.72
  (132 shorter events, 4.4 us)
Async XLA Ops:
  7.2 9.4 copy-start.41
  7.2 7.2 copy-start.9
  7.2 11.3 copy-start
  7.2 63.7 %all-gather.7.cloned.1.call-start = ((), (), s32[]{:S(2)}) async-start(), calls=%async_computation.6 | async-start | bytes 2162688 | tf_op jit(solution)/shard_map/all_gather | solution.py:144
  9.0 160.4 %all-gather.9.cloned.1.call-start = ((), (), s32[]{:S(2)}) async-start(), calls=%async_computation.7 | async-start | bytes 12976128 | tf_op jit(solution)/shard_map/all_gather | solution.py:143
  10.9 9.0 copy-start.31
  11.0 229.6 %all-gather.11.cloned.1.call-start = ((), (), s32[]{:S(2)}) async-start(), calls=%async_computation.8 | async-start | bytes 6488064 | tf_op jit(solution)/shard_map/all_gather | solution.py:155
  12.7 289.2 %all-gather.13.cloned.1.call-start = ((), (), s32[]{:S(2)}) async-start(), calls=%async_computation.9 | async-start | bytes 2162688 | tf_op jit(solution)/shard_map/all_gather | solution.py:156
  14.4 364.6 %all-gather.15.cloned.1.call-start = ((), (), s32[]{:S(2)}) async-start(), calls=%async_computation.10 | async-start | bytes 8650752 | tf_op jit(solution)/shard_map/all_gather | solution.py:172
  15.2 744.8 %reduce-scatter.13.cloned.1.call-start = ((), (), s32[]{:S(2)}) async-start(), calls=%async_computation.15 | async-start | bytes 17301504 | tf_op jit(solution)/shard_map/reduce_scatter | solution.py:193
  18.8 221.8 %copy-start.29 = (f32[680]{0:T(1024)}, f32[680]{0:T(1024)S(1)}, u32[]{:S(2)}) copy-start(f32[680]{0:T(1024)S(1)} %broadcast_multiply_fusion.3) | copy-start | bytes 8164
  19.3 0.6 copy-start.27
  19.9 220.7 %copy-start.23 = (f32[680]{0:T(1024)}, f32[680]{0:T(1024)S(1)}, u32[]{:S(2)}) copy-start(f32[680]{0:T(1024)S(1)} %fusion.56) | copy-start | bytes 8164
  73.2 102.4 %copy-start.25 = (f32[1,1024]{1,0:T(1,128)}, f32[1,1024]{1,0:T(1,128)S(1)}, u32[]{:S(2)}) copy-start(f32[1,1024]{1,0:T(1,128)S(1)} %fusion.87) | copy-start | bytes 12292
  175.7 74.8 %copy-start.32 = (f32[1,1024]{1,0:T(1,128)}, f32[1,1024]{1,0:T(1,128)S(1)}, u32[]{:S(2)}) copy-start(f32[1,1024]{1,0:T(1,128)S(1)} %get-tuple-element.113) | copy-start | bytes 12292
  175.7 74.8 %copy-start.36 = (f32[1,1024]{1,0:T(1,128)}, f32[1,1024]{1,0:T(1,128)S(1)}, u32[]{:S(2)}) copy-start(f32[1,1024]{1,0:T(1,128)S(1)} %get-tuple-element.112) | copy-start | bytes 12292
  175.7 203.3 %copy-start.17 = (f32[1,1024]{1,0:T(1,128)}, f32[1,1024]{1,0:T(1,128)S(1)}, u32[]{:S(2)}) copy-start(f32[1,1024]{1,0:T(1,128)S(1)} %get-tuple-element.115) | copy-start | bytes 12292
  379.0 13.2 copy-start.39
  388.1 4.0 copy-start.42
  403.9 356.1 %copy-start.16 = (f32[128,1024]{1,0:T(8,128)S(1)}, f32[128,1024]{1,0:T(8,128)}, u32[]{:S(2)}) copy-start(f32[128,1024]{1,0:T(8,128)} %param.31) | copy-start | bytes 1572868
  403.9 438.3 %all-gather.17.cloned.1.call-start = ((), (), s32[]{:S(2)}) async-start(), calls=%async_computation.11 | async-start | bytes 8650752 | tf_op jit(solution)/shard_map/all_gather | solution.py:173
  763.0 397.4 %reduce-scatter.17.cloned.1.call-start = ((), (), s32[]{:S(2)}) async-start(), calls=%async_computation.17 | async-start | bytes 4325376 | tf_op jit(solution)/shard_map/reduce_scatter | solution.py:232
  858.9 10.9 copy-start.5
  869.8 1.5 copy-start.3
  869.8 3.0 copy-start.38
  869.8 4.0 copy-start.40
  871.3 1.5 copy-start.8
  973.7 3.0 copy-start.1
  973.7 3.0 copy-start.30
  973.7 3.0 copy-start.33
  976.7 11.3 copy-start.6
  976.7 11.2 copy-start.28
  987.9 2.0 copy-start.24
  989.9 3.6 copy-start.2
  989.9 3.6 copy-start.4
  1009.9 7.9 copy-start.26
  1009.9 8.0 copy-start.34
  1020.2 281.2 %reduce-scatter.9.cloned.1.call-start = ((), (), s32[]{:S(2)}) async-start(), calls=%async_computation.13 | async-start | bytes 4325376 | tf_op jit(solution)/shard_map/reduce_scatter | solution.py:209
  1027.0 0.7 copy-start.37
  1027.0 432.5 %reduce-scatter.7.cloned.1.call-start = ((), (), s32[]{:S(2)}) async-start(), calls=%async_computation.12 | async-start | bytes 12976128 | tf_op jit(solution)/shard_map/reduce_scatter | solution.py:208
  1038.8 0.7 copy-start.18
  1038.8 779.6 %reduce-scatter.11.cloned.1.call-start = ((), (), s32[]{:S(2)}) async-start(), calls=%async_computation.14 | async-start | bytes 17301504 | tf_op jit(solution)/shard_map/reduce_scatter | solution.py:192
  1052.7 0.7 copy-start.35
  1052.7 1019.7 %reduce-scatter.15.cloned.1.call-start = ((), (), s32[]{:S(2)}) async-start(), calls=%async_computation.16 | async-start | bytes 25952256 | tf_op jit(solution)/shard_map/reduce_scatter | solution.py:231
  1064.9 95.5 %copy-start.14 = (f32[1000,32]{0,1:T(8,128)S(1)}, f32[1000,32]{0,1:T(8,128)}, u32[]{:S(2)}) copy-start(f32[1000,32]{0,1:T(8,128)} %param.33) | copy-start | bytes 384004
  1064.9 95.5 %copy-start.19 = (f32[1000,32]{0,1:T(8,128)S(1)}, f32[1000,32]{0,1:T(8,128)}, u32[]{:S(2)}) copy-start(f32[1000,32]{0,1:T(8,128)} %param.45) | copy-start | bytes 384004
  1064.9 95.5 %copy-start.20 = (f32[1000,32]{0,1:T(8,128)S(1)}, f32[1000,32]{0,1:T(8,128)}, u32[]{:S(2)}) copy-start(f32[1000,32]{0,1:T(8,128)} %param.39) | copy-start | bytes 384004
  1064.9 236.5 %copy-start.15 = (f32[32,1024]{1,0:T(8,128)S(1)}, f32[32,1024]{1,0:T(8,128)}, u32[]{:S(2)}) copy-start(f32[32,1024]{1,0:T(8,128)} %param.29) | copy-start | bytes 393220
  1065.0 236.5 %copy-start.21 = (f32[32,1024]{1,0:T(8,128)S(1)}, f32[32,1024]{1,0:T(8,128)}, u32[]{:S(2)}) copy-start(f32[32,1024]{1,0:T(8,128)} %param.41) | copy-start | bytes 393220
  1065.0 236.4 %copy-start.22 = (f32[32,1024]{1,0:T(8,128)S(1)}, f32[32,1024]{1,0:T(8,128)}, u32[]{:S(2)}) copy-start(f32[32,1024]{1,0:T(8,128)} %param.35) | copy-start | bytes 393220
  1065.0 394.5 %copy-start.11 = (f32[32,3072]{1,0:T(8,128)S(1)}, f32[32,3072]{1,0:T(8,128)}, u32[]{:S(2)}) copy-start(f32[32,3072]{1,0:T(8,128)} %param.28) | copy-start | bytes 1179652
  1065.0 753.3 %copy-start.10 = (f32[32,4096]{1,0:T(8,128)S(1)}, f32[32,4096]{1,0:T(8,128)}, u32[]{:S(2)}) copy-start(f32[32,4096]{1,0:T(8,128)} %param.30) | copy-start | bytes 1572868
  1303.1 769.2 %copy-start.7 = (f32[32,6144]{1,0:T(8,128)S(1)}, f32[32,6144]{1,0:T(8,128)}, u32[]{:S(2)}) copy-start(f32[32,6144]{1,0:T(8,128)} %param.32) | copy-start | bytes 2359300
  1303.1 769.2 %copy-start.12 = (f32[32,6144]{1,0:T(8,128)S(1)}, f32[32,6144]{1,0:T(8,128)}, u32[]{:S(2)}) copy-start(f32[32,6144]{1,0:T(8,128)} %param.44) | copy-start | bytes 2359300
  1303.1 769.2 %copy-start.13 = (f32[32,6144]{1,0:T(8,128)S(1)}, f32[32,6144]{1,0:T(8,128)}, u32[]{:S(2)}) copy-start(f32[32,6144]{1,0:T(8,128)} %param.38) | copy-start | bytes 2359300
Sparse Core Ops, SparseCore 0:
  11.7 59.1 all-gather.6
  74.4 94.8 all-gather.8
  172.8 67.7 all-gather.10
  244.1 54.9 all-gather.12
  302.7 76.2 all-gather.14
  404.0 355.9 reduce-scatter.12
  763.7 78.5 all-gather.16
  1020.4 140.0 reduce-scatter.16
  1162.7 138.6 reduce-scatter.8
  1307.3 152.1 reduce-scatter.6
  1461.9 356.4 reduce-scatter.10
  1825.8 246.5 reduce-scatter.14
where the time goes:
time: 2090 us; the launch traced here: 2080 us
  waiting for transfers between devices  1720 us (82%)
  matrix products  238 us (11%)
  other arithmetic  93.6 us (4%)
    reduce_scatter x1, waiting for transfers between devices, per_device(): lax.psum_scatter(grad_fc1, ('fsdp', 'grp'), scatter_dimension=0, tiled=True)  356 us
    reduce_scatter x1, waiting for transfers between devices, per_device(): lax.psum_scatter(grad_fc2, ('fsdp', 'grp'), scatter_dimension=0, tiled=True)  356 us
    reduce_scatter x1, waiting for transfers between devices, per_device(): lax.psum_scatter(grad_ada, ('fsdp', 'grp'), scatter_dimension=0, tiled=True)  251 us
    reduce_scatter x1, waiting for transfers between devices, per_device(): lax.psum_scatter(grad_qkv, ('fsdp', 'grp'), scatter_dimension=0, tiled=True)  156 us
    reduce_scatter x1, waiting for transfers between devices, per_device(): lax.psum_scatter(grad_proj, ('fsdp', 'grp'), scatter_dimension=0, tiled=T...  139 us
    all_gather x1, waiting for transfers between devices, per_device(): lax.all_gather(cast_ada, ('fsdp', 'grp'), axis=0, tiled=True)  95.5 us
    reduce_scatter x1, waiting for transfers between devices, per_device(): lax.psum_scatter(grad_table, ('fsdp', 'grp'), scatter_dimension=1, tiled=...  95.4 us
    all_gather x1, waiting for transfers between devices, per_device(): lax.all_gather(cast_fc2, ('fsdp', 'grp'), axis=0, tiled=True)  78.6 us
  transfers between devices with their start and end apart: 12, of which 11 were waited for; matrix products, arithmetic and copies ran while one was open for 7% of the time, Pallas kernels for 0%

commit v1 on v0

v1 whole, which is shorter than its diff:
```python
import functools

import jax
import jax.numpy as jnp
import numpy as np
from jax import lax
from jax.experimental import pallas as pl
from jax.experimental.pallas import tpu as pltpu
from jax.sharding import PartitionSpec as P

D = 1024
HEADS = 16
HEAD = 64
FF = 4096
SCALES = 10
STEP = 3
AXES = ("fsdp", "grp")

patch_sides = (1, 2, 3, 4, 5, 6, 8, 10, 13, 16)
norm_eps = 1e-06
adam_eps = 1e-08
decay = 0.05
highest = lax.Precision.HIGHEST
bf16 = jnp.bfloat16
f32 = jnp.float32


def scale_layout(slots):
    squares = np.array(patch_sides[:SCALES], dtype=np.int64) ** 2
    bounds = np.cumsum(squares)
    scale_ids = np.searchsorted(bounds, np.arange(slots), side="right")
    return (bounds.astype(np.int32), scale_ids.astype(np.int32))


def norm_rows(values):
    centre = values - jnp.mean(values, axis=-1, keepdims=True)
    spread = jnp.mean(centre * centre, axis=-1, keepdims=True)
    return centre * lax.rsqrt(spread + norm_eps)


def modulate(values, scale_row, shift_row):
    return norm_rows(values) * (1.0 + scale_row) + shift_row


def gelu_tanh(values):
    return jax.nn.gelu(values, approximate=True)


def learn_rates():
    return (D ** (-0.5), (D // 16) ** (-0.5), D ** (-0.5), FF ** (-0.5), D ** (-0.5), 1.0)


def adamw(weight, gradient, first, second, bias_one, bias_two, rate):
    first_new = 0.5 * first + 0.5 * gradient
    second_new = 0.5 * second + 0.5 * gradient * gradient
    update = first_new / bias_one / (jnp.sqrt(second_new / bias_two) + adam_eps) + decay * weight
    weight_new = weight - rate * update
    return (weight_new, weight_new.astype(bf16), first_new, second_new)


def contract_rows(former, latter):
    return lax.dot_general(former, latter, (((0,), (0,)), ((), ())), preferred_element_type=f32)


def contract_cols(former, latter):
    return lax.dot_general(former, latter, (((1,), (1,)), ((), ())), preferred_element_type=f32)


def dot_nt(former, latter):
    return lax.dot_general(former, latter, (((1,), (1,)), ((), ())), preferred_element_type=f32)


def dot_nn(former, latter):
    return lax.dot_general(former, latter, (((1,), (0,)), ((), ())), preferred_element_type=f32)


def dot_tn(former, latter):
    return lax.dot_general(former, latter, (((0,), (0,)), ((), ())), preferred_element_type=f32)


FORWARD_TILES = ((0, 240, 256), (240, 416, 432), (416, 680, 680))
BACKWARD_TILES = ((0, 128, 160), (128, 384, 432), (384, 680, 680))


def attend_kernel(q_ref, k_ref, v_ref, bias_ref, context_ref, lse_ref):
    for begin, end, keys in FORWARD_TILES:
        q = q_ref[begin:end, :] * bf16(0.125)
        lane = lax.broadcasted_iota(jnp.int32, q.shape, 1)
        contexts, totals = [], []
        for head in range(2):
            own = jnp.where((lane < HEAD) == (head == 0), q, bf16(0))
            scores = dot_nt(own, k_ref[:keys, :]) + bias_ref[begin:end, :keys]
            largest = jnp.max(scores, axis=1, keepdims=True)
            expo = jnp.exp(scores - largest)
            total = jnp.sum(expo, axis=1, keepdims=True)
            probs = (expo * (1.0 / total)).astype(bf16)
            totals.append(largest + jnp.log(total))
            contexts.append(dot_nn(probs, v_ref[:keys, :]))
        left = lax.broadcasted_iota(jnp.int32, contexts[0].shape, 1) < HEAD
        context_ref[begin:end, :] = jnp.where(left, contexts[0], contexts[1]).astype(bf16)
        lse = jnp.where(left, totals[0], totals[1]).T
        lse_ref[0, 0:1, begin:end] = lse[0:1]
        lse_ref[0, 1:2, begin:end] = lse[HEAD : HEAD + 1]


def attend_forward(packed, bias):
    slots, width = packed.shape[0], packed.shape[1] // 3
    pairs = width // 128
    assert slots == FORWARD_TILES[-1][1]

    def block(offset):
        return pl.BlockSpec((slots, 128), lambda i: (0, offset + i))

    return pl.pallas_call(
        attend_kernel,
        grid=(pairs,),
        in_specs=[
            block(0),
            block(pairs),
            block(2 * pairs),
            pl.BlockSpec((slots, slots), lambda i: (0, 0)),
        ],
        out_specs=[block(0), pl.BlockSpec((1, 2, slots), lambda i: (i, 0, 0))],
        out_shape=[
            jax.ShapeDtypeStruct((slots, width), bf16),
            jax.ShapeDtypeStruct((pairs, 2, slots), f32),
        ],
        cost_estimate=pl.CostEstimate(
            flops=10 * slots * slots * width,
            bytes_accessed=12 * slots * width,
            transcendentals=slots * slots * HEADS,
        ),
        compiler_params=pltpu.CompilerParams(vmem_limit_bytes=48 << 20),
        name="attend",
    )(packed, packed, packed, bias)


def attend_back_kernel(
    q_ref, k_ref, v_ref, grad_ref, lse_ref, bias_ref, out_ref, keys_ref, values_ref
):
    for count, (begin, end, keys) in enumerate(reversed(BACKWARD_TILES)):
        q = q_ref[begin:end, :] * bf16(0.125)
        grad = grad_ref[begin:end, :]
        k = k_ref[:keys, :]
        v = v_ref[:keys, :]
        left = lax.broadcasted_iota(jnp.int32, q.shape, 1) < HEAD
        d_q, d_k, d_v = [], [], []
        for head in range(2):
            own = left == (head == 0)
            scores = dot_nt(k, jnp.where(own, q, bf16(0))) + bias_ref[:keys, begin:end]
            probs = jnp.exp(scores - lse_ref[0, head : head + 1, begin:end])
            d_probs = dot_nt(v, jnp.where(own, grad, bf16(0)))
            inner = jnp.sum(probs * d_probs, axis=0, keepdims=True)
            d_scores = (probs * (d_probs - inner)).astype(bf16)
            d_v.append(dot_nn(probs.astype(bf16), grad))
            d_k.append(dot_nn(d_scores, q))
            d_q.append(dot_tn(d_scores, k))
        first = lax.broadcasted_iota(jnp.int32, d_k[0].shape, 1) < HEAD
        d_k = jnp.where(first, d_k[0], d_k[1])
        d_v = jnp.where(first, d_v[0], d_v[1])
        if count == 0:
            keys_ref[:keys, :] = d_k
            values_ref[:keys, :] = d_v
        else:
            keys_ref[:keys, :] += d_k
            values_ref[:keys, :] += d_v
        out_ref[0, begin:end, :] = (jnp.where(left, d_q[0], d_q[1]) * 0.125).astype(bf16)
    out_ref[1] = keys_ref[...].astype(bf16)
    out_ref[2] = values_ref[...].astype(bf16)


def attend_backward(packed, d_context, lse, bias_t):
    slots, width = packed.shape[0], packed.shape[1] // 3
    pairs = width // 128
    assert slots == BACKWARD_TILES[-1][1]

    def block(offset):
        return pl.BlockSpec((slots, 128), lambda i: (0, offset + i))

    return pl.pallas_call(
        attend_back_kernel,
        grid=(pairs,),
        in_specs=[
            block(0),
            block(pairs),
            block(2 * pairs),
            block(0),
            pl.BlockSpec((1, 2, slots), lambda i: (i, 0, 0)),
            pl.BlockSpec((slots, slots), lambda i: (0, 0)),
        ],
        out_specs=pl.BlockSpec((3, slots, 128), lambda i: (0, 0, i)),
        out_shape=jax.ShapeDtypeStruct((3, slots, width), bf16),
        scratch_shapes=[pltpu.VMEM((slots, 128), f32), pltpu.VMEM((slots, 128), f32)],
        cost_estimate=pl.CostEstimate(
            flops=20 * slots * slots * width,
            bytes_accessed=16 * slots * width,
            transcendentals=slots * slots * HEADS,
        ),
        compiler_params=pltpu.CompilerParams(vmem_limit_bytes=56 << 20),
        name="attend_back",
    )(packed, packed, packed, d_context, lse, bias_t)


def gather_kernel(layout, place_ref, x_ref, *refs):
    depth, rows, left, half, chunk, gelu = layout
    outs = 2 if gelu else 1
    pieces, whole_ref, out_refs = refs[:8], refs[8], refs[9 : 9 + outs]
    w_ref, y_refs = refs[9 + outs], refs[10 + outs : 10 + 2 * outs]
    in_sems, whole_sems, out_sems = refs[10 + 2 * outs :]
    z, x, c, y = [place_ref[i] for i in range(4)]
    for color in range(2):
        for far in range(2):
            for core in range(2):
                piece = pieces[core * 4 + far * 2 + color]
                for near in range(2):
                    step_x, step_y = (far, near) if color == 0 else (near, far)
                    for step in range(depth):
                        at = lax.rem(z + depth - step, depth) * 2 + (x ^ step_x)
                        at = (at * 2 + (c ^ core)) * 2 + (y ^ step_y)
                        at = pl.multiple_of(at * rows, rows)
                        pltpu.make_async_copy(
                            piece.at[near, step, :, pl.ds(left, half)],
                            w_ref.at[color, pl.ds(at, rows), :],
                            in_sems.at[color],
                        ).start()
    waits = []
    for color in range(2):
        own = w_ref.at[color]
        pltpu.make_async_copy(own, own, in_sems.at[color]).wait()
        copy = pltpu.make_async_copy(
            own, whole_ref.at[:, pl.ds(color * half, half)], whole_sems.at[color]
        )
        copy.start()
        waits.append(copy)
        for begin in range(0, half, chunk):
            at = color * half + begin
            result = dot_nn(x_ref[...], w_ref[color, :, begin : begin + chunk])
            values = [result, gelu_tanh(result)] if gelu else [result]
            for i, value in enumerate(values):
                y_refs[i][:, at : at + chunk] = value.astype(y_refs[i].dtype)
                copy = pltpu.make_async_copy(
                    y_refs[i].at[:, pl.ds(at, chunk)],
                    out_refs[i].at[:, pl.ds(at, chunk)],
                    out_sems.at[i, at // chunk],
                )
                copy.start()
                waits.append(copy)
    for copy in waits:
        copy.wait()


def gather_dot(place, x, pieces, left, half, kinds, name):
    depth, rows = pieces[0].shape[1:3]
    whole, width = rows * depth * 8, 2 * half
    slots = x.shape[0]
    chunk = min(512, half)
    anywhere = pl.BlockSpec(memory_space=pl.ANY)
    return pl.pallas_call(
        functools.partial(gather_kernel, (depth, rows, left, half, chunk, len(kinds) == 2)),
        grid_spec=pltpu.PrefetchScalarGridSpec(
            num_scalar_prefetch=1,
            grid=(1,),
            in_specs=[pl.BlockSpec(x.shape, lambda i, place: (0, 0))] + [anywhere] * 8,
            out_specs=[anywhere] * (1 + len(kinds)),
            scratch_shapes=[pltpu.VMEM((2, whole, half), bf16)]
            + [pltpu.VMEM((slots, width), kind) for kind in kinds]
            + [
                pltpu.SemaphoreType.DMA((2,)),
                pltpu.SemaphoreType.DMA((2,)),
                pltpu.SemaphoreType.DMA((len(kinds), width // chunk)),
            ],
        ),
        out_shape=[jax.ShapeDtypeStruct((whole, width), bf16)]
        + [jax.ShapeDtypeStruct((slots, width), kind) for kind in kinds],
        cost_estimate=pl.CostEstimate(
            flops=3 * slots * whole * width,
            bytes_accessed=4 * whole * width + 4 * slots * width,
            transcendentals=0,
        ),
        compiler_params=pltpu.CompilerParams(vmem_limit_bytes=60 << 20),
        name=name,
    )(place, x, *pieces)


def gelu_back_kernel(half, place_ref, grad_ref, weight_ref, inner_ref, out_ref, give_ref):
    d_act = dot_nt(grad_ref[...], weight_ref[...])
    _, back = jax.vjp(gelu_tanh, inner_ref[...])
    value = back(d_act)[0].astype(bf16)
    out_ref[...] = value

    @pl.when(pl.program_id(0) < half)
    def _():
        give_ref[...] = value


def gelu_back_dot(place, grad, weight, inner):
    slots, width = inner.shape
    chunk = 512
    half = width // chunk // 2

    def at(i, place):
        return lax.rem(i + (1 - place[2]) * half, 2 * half)

    return pl.pallas_call(
        functools.partial(gelu_back_kernel, half),
        grid_spec=pltpu.PrefetchScalarGridSpec(
            num_scalar_prefetch=1,
            grid=(2 * half,),
            in_specs=[
                pl.BlockSpec(grad.shape, lambda i, place: (0, 0)),
                pl.BlockSpec((chunk, weight.shape[1]), lambda i, place: (at(i, place), 0)),
                pl.BlockSpec((slots, chunk), lambda i, place: (0, at(i, place))),
            ],
            out_specs=[
                pl.BlockSpec((slots, chunk), lambda i, place: (0, at(i, place))),
                pl.BlockSpec((slots, chunk), lambda i, place: (0, jnp.minimum(i, half - 1))),
            ],
        ),
        out_shape=[
            jax.ShapeDtypeStruct((slots, width), bf16),
            jax.ShapeDtypeStruct((slots, width // 2), bf16),
        ],
        cost_estimate=pl.CostEstimate(
            flops=3 * slots * width * weight.shape[1],
            bytes_accessed=8 * slots * width + 2 * width * weight.shape[1],
            transcendentals=slots * width,
        ),
        compiler_params=pltpu.CompilerParams(vmem_limit_bytes=48 << 20),
        name="gelu_back",
    )(place, grad, weight, inner)


def weight_grad_kernel(
    depth, rows, chunks, place_ref, own_ref, other_ref, mine_ref, take_ref, *out_refs
):
    step = pl.program_id(0)
    total = dot_tn(own_ref[...], mine_ref[0]) + dot_tn(other_ref[...], take_ref[0])
    total = total.reshape(depth, 2, 2, 2, rows, total.shape[-1])

    @pl.when(step < chunks // 2)
    def _():
        low, high = total[:, :, :, 0], total[:, :, :, 1]
        first = place_ref[3] == 0
        out_refs[0][...] = jnp.where(first, high, low).astype(bf16)
        out_refs[1][...] = jnp.where(first, low, high).astype(bf16)

    @pl.when(step >= chunks // 2)
    def _():
        low, high = total[:, 0], total[:, 1]
        first = place_ref[1] == 0
        out_refs[2][...] = jnp.where(first, high, low).astype(bf16)
        out_refs[3][...] = jnp.where(first, low, high).astype(bf16)


def weight_grad_call(place, own, other, rhs, take, rows):
    groups, slots, columns = rhs.shape
    half, width = columns // 2, own.shape[1]
    depth = width // rows // 8
    chunk = 512 if half % 1024 == 0 else 256
    per = half // chunk
    chunks = groups * per
    assert chunks % 2 == 0
    turn = chunks // 2
    all_rows = pl.BlockSpec(own.shape, lambda i, place: (0, 0))
    block = (depth, 2, 2, rows, chunk)
    early = pl.BlockSpec(block, lambda i, place: (0, 0, 0, 0, jnp.minimum(i, turn - 1)))
    late = pl.BlockSpec(block, lambda i, place: (0, 0, 0, 0, jnp.maximum(i - turn, 0)))
    shape = jax.ShapeDtypeStruct((depth, 2, 2, rows, groups * half // 2), bf16)
    return pl.pallas_call(
        functools.partial(weight_grad_kernel, depth, rows, chunks),
        grid_spec=pltpu.PrefetchScalarGridSpec(
            num_scalar_prefetch=1,
            grid=(chunks,),
            in_specs=[
                all_rows,
                all_rows,
                pl.BlockSpec(
                    (1, slots, chunk), lambda i, place: (i // per, 0, place[2] * per + i % per)
                ),
                pl.BlockSpec((1, slots, chunk), lambda i, place: (i // per, 0, i % per)),
            ],
            out_specs=[early, early, late, late],
        ),
        out_shape=[shape] * 4,
        cost_estimate=pl.CostEstimate(
            flops=6 * slots * width * groups * half,
            bytes_accessed=4 * slots * (width + groups * half) + 2 * width * groups * half,
            transcendentals=0,
        ),
        compiler_params=pltpu.CompilerParams(vmem_limit_bytes=60 << 20),
        name="weight_grad",
    )(place, own, other, rhs, take)


class Grid:
    def __init__(self, fsdp, grp):
        outer = fsdp // 2
        self.size = {"c": 2, "x": 2 if outer % 2 == 0 else 1, "y": grp}
        self.size["z"] = outer // self.size["x"]
        self.count = fsdp * grp
        self.fsdp = fsdp

    def here(self):
        place = lax.axis_index("fsdp")
        wide = self.size["x"]
        return {
            "c": place % 2,
            "x": (place // 2) % wide,
            "z": place // (2 * wide),
            "y": lax.axis_index("grp"),
        }

    def shift(self, array, axis, step):
        size = self.size[axis]
        if axis == "y":
            return lax.ppermute(array, "grp", [(i, (i + step) % size) for i in range(size)])
        stride = {"c": 1, "x": 2, "z": 2 * self.size["x"]}[axis]
        pairs = []
        for i in range(self.fsdp):
            at = (i // stride) % size
            pairs.append((i, i + ((at + step) % size - at) * stride))
        return lax.ppermute(array, "fsdp", pairs)

    def fits(self, rows):
        return self.size["x"] == 2 and self.size["y"] == 2 and rows % 32 == 0

    def gather_line(self, shards):
        lows = [shard[:, : shard.shape[1] // 2] for shard in shards]
        highs = [shard[:, shard.shape[1] // 2 :] for shard in shards]
        shard = jnp.concatenate(lows + highs, axis=1)
        half = shard.shape[1] // 2
        steps = [shard] + [self.shift(shard, "z", step) for step in range(1, self.size["z"])]
        return [jnp.stack([p[:, i * half : (i + 1) * half] for p in steps]) for i in range(2)]

    def gather_plane(self, line):
        orders = ("yx", "xy")
        plane = [
            jnp.stack([own, self.shift(own, order[0], 1)]) for own, order in zip(line, orders)
        ]
        far = [self.shift(own, order[1], 1) for own, order in zip(plane, orders)]
        mine = plane + far
        return mine + [self.shift(piece, "c", 1) for piece in mine]

    def scatter_sum(self, array, axis, dim, here, kind=bf16):
        size = self.size[axis]
        total = lax.dynamic_index_in_dim(array, here[axis], dim, keepdims=False)
        for step in range(1, size):
            piece = lax.dynamic_index_in_dim(array, (here[axis] + step) % size, dim, keepdims=False)
            total = total + self.shift(piece.astype(kind), axis, step).astype(f32)
        return total


def per_device(
    grid,
    block_in,
    cotangent,
    stop_scale,
    class_label,
    w_qkv,
    w_proj,
    w_fc1,
    w_fc2,
    w_ada,
    w_table,
    m_qkv,
    m_proj,
    m_fc1,
    m_fc2,
    m_ada,
    m_table,
    v_qkv,
    v_proj,
    v_fc1,
    v_fc2,
    v_ada,
    v_table,
):
    items, slots, width = block_in.shape
    assert items == 1
    here = grid.here()
    bounds, scale_ids = scale_layout(slots)
    picked = jnp.arange(SCALES) == stop_scale[0] - 1
    length = jnp.sum(jnp.where(picked, jnp.asarray(bounds), 0))
    position = jnp.arange(slots)
    valid = (position < length).astype(f32)[:, None]
    scale_table = jnp.asarray(scale_ids)
    allowed = (scale_table[None, :] <= scale_table[:, None]) & (position[None, :] < length)
    bias = jnp.where(allowed, f32(0), f32(-1e30))
    bias_t = bias.T
    place = jnp.stack([here[axis] for axis in "zxcy"]).astype(jnp.int32)
    fits = grid.fits(w_qkv.shape[0])
    cast_qkv, cast_proj, cast_fc1, cast_fc2 = [
        w.astype(bf16) for w in (w_qkv, w_proj, w_fc1, w_fc2)
    ]
    half_qkv, half_proj, half_fc1 = [w.shape[1] // 2 for w in (w_qkv, w_proj, w_fc1)]
    labels = lax.all_to_all(
        jnp.broadcast_to(class_label, (grid.count,)), AXES, 0, 0, tiled=True
    )
    cast_ada = w_ada.astype(bf16)
    cast_table = w_table.astype(bf16)
    onehot = (labels[:, None] == jnp.arange(cast_table.shape[0])[None, :]).astype(bf16)
    cond = jnp.dot(onehot, cast_table, preferred_element_type=f32)
    silu_out, silu_back = jax.vjp(jax.nn.silu, cond)
    lifted_low = silu_out.astype(bf16)

    def ada_part(begin, end):
        return jnp.dot(lifted_low, cast_ada[:, begin:end], preferred_element_type=f32)

    def ada_sum(part):
        mine = lax.all_to_all(part, AXES, 0, 0, tiled=True)
        return jnp.sum(mine, axis=0, keepdims=True)

    early = ada_part(width, 3 * width)
    late = jnp.concatenate([ada_part(0, width), ada_part(3 * width, 6 * width)], axis=1)
    if fits:
        line_qkv = grid.gather_line([cast_qkv])
        line_qkv, cast_proj, cast_fc1, early = lax.optimization_barrier(
            (line_qkv, cast_proj, cast_fc1, early)
        )
        line_rest = grid.gather_line([cast_proj, cast_fc1])
        pieces_qkv = grid.gather_plane(line_qkv)
    early = ada_sum(early)
    if fits:
        line_rest, cast_fc2, early, late, _ = lax.optimization_barrier(
            (line_rest, cast_fc2, early, late, pieces_qkv[2:4])
        )
        pieces_rest = grid.gather_plane(line_rest)
        line_fc2 = grid.gather_line([cast_fc2])
        line_fc2, _ = lax.optimization_barrier((line_fc2, pieces_rest[2:4]))
        pieces_fc2 = grid.gather_plane(line_fc2)
    late = ada_sum(late)
    scale_one, shift_one = early[:, :width], early[:, width:]
    gamma_one, gamma_two, scale_two, shift_two = [
        late[:, i * width : (i + 1) * width] for i in range(4)
    ]

    def weight_grad(lhs, rhs, other_lhs, give=None):
        groups, _, columns = rhs.shape
        half = columns // 2
        size = grid.size
        rows = lhs.shape[1] // grid.count
        if give is None:
            give = lax.dynamic_slice_in_dim(rhs, (1 - here["c"]) * half, half, 2)
        take = grid.shift(give, "c", 1)
        if grid.fits(rows):
            away_one, one, away_two, two = weight_grad_call(place, lhs, other_lhs, rhs, take, rows)
            first = away_one
            one = one.astype(f32) + grid.shift(away_one, "y", 1).astype(f32)
            two = two.astype(f32) + grid.shift(away_two, "x", 1).astype(f32)
        else:
            mine = lax.dynamic_slice_in_dim(rhs, here["c"] * half, half, 2)
            both = jnp.concatenate([mine, take], axis=1)
            both = jnp.concatenate([both[i] for i in range(groups)], axis=1)
            grad = contract_rows(jnp.concatenate([lhs, other_lhs], axis=0), both)
            first = grad
            grad = grad.reshape(size["z"], size["x"], 2, size["y"], rows, groups * half)
            middle = groups * half // 2
            one = grid.scatter_sum(grad[..., :middle], "y", 3, here)
            two = grid.scatter_sum(grad[..., middle:], "x", 1, here)
        one = grid.scatter_sum(one, "x", 1, here)
        two = grid.scatter_sum(two, "y", 2, here)
        both = grid.scatter_sum(jnp.concatenate([one, two], axis=-1), "z", 0, here)
        keep = lax.dynamic_index_in_dim(both, here["c"], 0, keepdims=False)
        give = lax.dynamic_index_in_dim(both, 1 - here["c"], 0, keepdims=False)
        take = grid.shift(give, "c", 1)
        low = jnp.where(here["c"] == 0, keep, take).reshape(rows, groups, 1, half)
        high = jnp.where(here["c"] == 0, take, keep).reshape(rows, groups, 1, half)
        return jnp.concatenate([low, high], axis=2).reshape(rows, groups * columns), first

    tokens = block_in[0].astype(f32)
    hidden, modulate_one = jax.vjp(modulate, tokens, scale_one, shift_one)
    hidden_low = hidden.astype(bf16)
    hidden_other = grid.shift(hidden_low, "c", 1)
    if fits:
        wide_qkv, packed = gather_dot(
            place, hidden_low, pieces_qkv, 0, half_qkv, [bf16], "gather_qkv"
        )
    else:
        wide_qkv = lax.all_gather(cast_qkv, AXES, axis=0, tiled=True)
        packed = jnp.dot(hidden_low, wide_qkv, preferred_element_type=f32).astype(bf16)
    context, lse = attend_forward(packed, bias)
    context_other = grid.shift(context, "c", 1)
    if fits:
        wide_proj, attended = gather_dot(
            place, context, pieces_rest, 0, half_proj, [f32], "gather_proj"
        )
    else:
        wide_proj = lax.all_gather(cast_proj, AXES, axis=0, tiled=True)
        attended = jnp.dot(context, wide_proj, preferred_element_type=f32)
    middle = tokens + gamma_one * attended
    second, modulate_two = jax.vjp(modulate, middle, scale_two, shift_two)
    second_low = second.astype(bf16)
    second_other = grid.shift(second_low, "c", 1)
    if fits:
        wide_fc1, inner, activated_low = gather_dot(
            place, second_low, pieces_rest, half_proj, half_fc1, [f32, bf16], "gather_fc1"
        )
    else:
        wide_fc1 = lax.all_gather(cast_fc1, AXES, axis=0, tiled=True)
        inner = jnp.dot(second_low, wide_fc1, preferred_element_type=f32)
        activated_low = gelu_tanh(inner).astype(bf16)
    activated_other = grid.shift(activated_low, "c", 1)
    if fits:
        wide_fc2, branch = gather_dot(
            place, activated_low, pieces_fc2, 0, width // 2, [f32], "gather_fc2"
        )
    else:
        wide_fc2 = lax.all_gather(cast_fc2, AXES, axis=0, tiled=True)
        branch = jnp.dot(activated_low, wide_fc2, preferred_element_type=f32)
    block_out = ((middle + gamma_two * branch) * valid).astype(bf16)
    upstream = cotangent[0].astype(f32) * valid
    d_gamma_two = jnp.sum(upstream * branch, axis=0, keepdims=True)
    d_branch = (upstream * gamma_two).astype(bf16)
    sum_fc2, begun = weight_grad(activated_low, d_branch[None], activated_other)
    d_branch, _ = lax.optimization_barrier((d_branch, begun))
    d_inner_low, give = gelu_back_dot(place, d_branch, wide_fc2, inner)
    d_second = contract_cols(d_inner_low, wide_fc1)
    sum_fc1, begun = weight_grad(second_low, d_inner_low[None], second_other, give[None])
    d_second, _ = lax.optimization_barrier((d_second, begun))
    d_middle_part, d_scale_two, d_shift_two = modulate_two(d_second)
    d_middle = upstream + d_middle_part
    d_gamma_one = jnp.sum(d_middle * attended, axis=0, keepdims=True)
    d_attended = (d_middle * gamma_one).astype(bf16)
    d_context = contract_cols(d_attended, wide_proj).astype(bf16)
    sum_proj, begun = weight_grad(context, d_attended[None], context_other)
    d_context, _ = lax.optimization_barrier((d_context, begun))
    d_packed = attend_backward(packed, d_context, lse, bias_t)
    sum_qkv, begun = weight_grad(hidden_low, d_packed, hidden_other)
    d_packed, _ = lax.optimization_barrier((d_packed, begun))
    d_packed = jnp.concatenate([d_packed[0], d_packed[1], d_packed[2]], axis=1)
    d_hidden = contract_cols(d_packed, wide_qkv)
    d_tokens, d_scale_one, d_shift_one = modulate_one(d_hidden)
    grad_in = d_middle + d_tokens
    d_ada = jnp.concatenate(
        [d_gamma_one, d_scale_one, d_shift_one, d_gamma_two, d_scale_two, d_shift_two], axis=1
    ).astype(bf16)
    every_ada = lax.all_to_all(
        jnp.broadcast_to(d_ada, (grid.count, 6 * width)), AXES, 0, 0, tiled=True
    )
    sum_ada = contract_rows(lifted_low, every_ada)
    (d_cond,) = silu_back(contract_cols(every_ada, cast_ada))
    sum_table = lax.dot_general(
        onehot.astype(f32), d_cond, (((0,), (0,)), ((), ())), precision=highest
    )
    counter = f32(STEP)
    bias_one = 1.0 - jnp.power(f32(0.5), counter)
    bias_two = 1.0 - jnp.power(f32(0.5), counter)
    rates = learn_rates()
    updates = [
        adamw(w, g, m, v, bias_one, bias_two, rate)
        for w, g, m, v, rate in zip(
            (w_qkv, w_proj, w_fc1, w_fc2, w_ada, w_table),
            (sum_qkv, sum_proj, sum_fc1, sum_fc2, sum_ada, sum_table),
            (m_qkv, m_proj, m_fc1, m_fc2, m_ada, m_table),
            (v_qkv, v_proj, v_fc1, v_fc2, v_ada, v_table),
            rates,
        )
    ]
    return (block_out[None], grad_in[None]) + tuple(
        update[kind] for kind in range(4) for update in updates
    )


def solution(mesh):
    grid = Grid(mesh.shape["fsdp"], mesh.shape["grp"])
    items = P(AXES, None, None)
    vector = P(AXES)
    rows = P(AXES, None)
    columns = P(None, AXES)
    weights = (rows, rows, rows, rows, rows, columns)

    def run(*arrays):
        return per_device(grid, *arrays)

    return jax.shard_map(
        run,
        mesh=mesh,
        in_specs=(items, items, vector, vector) + weights * 3,
        out_specs=(items, items) + weights * 4,
        check_vma=False,
    )
```

time: 2090 us -> 586 us (0.28)
  waiting for transfers between devices: 1720 us -> 220 us
  matrix products: 238 us -> 25.7 us
  Pallas kernels: 0 us -> 159 us
  starting transfers between devices: 0.75 us -> 76.3 us
  other arithmetic: 93.6 us -> 65.1 us
    reduce_scatter x6 -> x0, waiting for transfers between devices: 1350 us -> none  [the longest x1 356 us: per_device(): lax.psum_scatter(grad_fc1, ('fsdp', 'grp'), scatter_dimension=0, tiled=True)]
    all_gather x6 -> x0, waiting for transfers between devices: 361 us -> none  [the longest x1 95.5 us: per_device(): lax.all_gather(cast_ada, ('fsdp', 'grp'), axis=0, tiled=True)]
    ppermute x0 -> x73, waiting for transfers between devices: none -> 202 us  [the longest x59 160 us: shift(): return lax.ppermute(array, 'fsdp', pairs)]
    pallas_call x0 -> x11, Pallas kernels: none -> 159 us  [the longest x4 45.2 us: weight_grad_call(): pl.pallas_call(functools.partial(weight_grad_kernel, depth, rows, chunks)...]
    dot_general x12 -> x5, matrix products: 146 us -> 2.41 us  [the longest x1 1.12 us: per_device(): lax.dot_general(onehot.astype(f32), d_cond, (((0,), (0,)), ((), ())), pre...]
    ppermute x0 -> x73, starting transfers between devices: none -> 60.4 us  [the longest x59 46.5 us: shift(): return lax.ppermute(array, 'fsdp', pairs)]
    dot_general x4 -> x1, matrix products: 42.7 us -> 2.34 us  [contract_rows(): lax.dot_general(former, latter, (((0,), (0,)), ((), ())), preferred_eleme...]
    convert_element_type x14 -> x19, other arithmetic: 53.6 us -> 19.4 us  [the longest x4 6.3 us: adamw(): return (weight_new, weight_new.astype(bf16), first_new, second_new)]
  transfers between devices with their start and end apart: 12 -> 77, of which waited for: 11 -> 31; matrix products, arithmetic and copies ran while one was open for 7% -> 16% of each run, Pallas kernels for 0% -> 22%
where the time goes in v1:
time: 586 us; the launch traced here: 579 us
  waiting for transfers between devices  220 us (38%)
  Pallas kernels  159 us (27%)
  starting transfers between devices  76.3 us (13%)
  other arithmetic  65.1 us (11%)
  local copies, waits for them, and re-layouts  28.8 us (5%)
  matrix products  25.7 us (4%)
    ppermute x59, waiting for transfers between devices, shift(): return lax.ppermute(array, 'fsdp', pairs)  160 us
    ppermute x59, starting transfers between devices, shift(): return lax.ppermute(array, 'fsdp', pairs)  46.5 us
    pallas_call x4, Pallas kernels, weight_grad_call(): pl.pallas_call(functools.partial(weight_grad_kernel, depth, rows, chunks)...  45.2 us
    pallas_call x4, Pallas kernels, gather_dot(): pl.pallas_call(functools.partial(gather_kernel, (depth, rows, left, half,...  43.2 us
    ppermute x14, waiting for transfers between devices, shift(): lax.ppermute(array, 'grp', [(i, (i + step) % size) for i in range(size)])  42.7 us
    pallas_call x1, Pallas kernels, attend_backward(): pl.pallas_call(attend_back_kernel, grid=(pairs,), in_specs=[block(0), blo...  30.4 us
    pallas_call x1, Pallas kernels, attend_forward(): pl.pallas_call(attend_kernel, grid=(pairs,), in_specs=[block(0), block(pa...  22.3 us
    dot_general x4, matrix products, contract_cols(): lax.dot_general(former, latter, (((1,), (1,)), ((), ())), preferred_eleme...  21 us
  transfers between devices with their start and end apart: 77, of which 31 were waited for; matrix products, arithmetic and copies ran while one was open for 16% of the time, Pallas kernels for 22%

profile of v1, /device:TPU:0, one launch (start us, length us, event | category | flops | bytes accessed | tf_op | source)
XLA Modules:
  0.0 578.6 jit_solution(8357864646977270353)
XLA Ops:
  1.8 5.1 collective-permute-start.2
  9.2 5.1 all-to-all-start
  18.3 7.4 %all-to-all-done = s32[32,1,1]{2,1,0:T(1,128)S(1)} async-done(((s32[32,1,1]{2,1,0:T(1,128)}), s32[32,1,1]{2,1,0:T(1,128)S(1)}, u32[]{:S(2)}, u32[]{:S(2)}) %all-to-all-start) | async-done | bytes 160 | tf_op jit(solution)/shard_map/all_to_all | solution.py:496
  28.8 3.8 collective-permute-start.5
  34.8 3.1 all-to-all-start.1
  37.9 1.8 collective-permute-start.6
  42.2 22.0 %collective-permute-done.4 = bf16[32,5120]{1,0:T(8,128)(2,1)S(1)} collective-permute-done((bf16[32,5120]{1,0:T(8,128)(2,1)S(1)}, bf16[32,5120]{1,0:T(8,128)(2,1)S(1)}, u32[]{:S(2)}, u32[]{:S(2)}) %collective-permute-start.4) | collective-permute-done | bytes 327712 | tf_op jit(solution)/shard_map/ppermute | solution.py:422
  67.7 15.6 %collective-permute-done.7.refs_2_ = bf16[2,4,32,1536]{3,2,1,0:T(8,128)(2,1)} collective-permute-done((bf16[2,4,32,1536]{3,2,1,0:T(8,128)(2,1)}, bf16[2,4,32,1536]{3,2,1,0:T(8,128)(2,1)}, u32[]{:S(2)}, u32[]{:S(2)}) %collective-permute-start.7) | collective-permute-done | bytes 786464 | tf_op jit(solution)/shard_map/ppermute | solution.py:422
  88.9 9.6 %collective-permute-done.14 = bf16[4,32,2560]{2,1,0:T(8,128)(2,1)S(1)} collective-permute-done((bf16[4,32,2560]{2,1,0:T(8,128)(2,1)S(1)}, bf16[4,32,2560]{2,1,0:T(8,128)(2,1)S(1)}, u32[]{:S(2)}, u32[]{:S(2)}) %collective-permute-start.14) | collective-permute-done | bytes 655392 | tf_op jit(solution)/shard_map/ppermute | solution.py:416
  104.0 2.1 and_select_fusion
  107.8 2.4 copy.86
  110.2 3.9 all-to-all-start.2
  114.7 19.3 %collective-permute-done.16.refs_2_ = bf16[2,4,32,2560]{3,2,1,0:T(8,128)(2,1)} collective-permute-done((bf16[2,4,32,2560]{3,2,1,0:T(8,128)(2,1)}, bf16[2,4,32,2560]{3,2,1,0:T(8,128)(2,1)}, u32[]{:S(2)}, u32[]{:S(2)}) %collective-permute-start.16) | collective-permute-done | bytes 1310752 | tf_op jit(solution)/shard_map/ppermute | solution.py:422
  136.4 9.6 %gather_qkv.1 = (bf16[1024,3072]{1,0:T(8,128)(2,1)}, bf16[680,3072]{1,0:T(8,128)(2,1)}) custom-call(s32[4]{0:T(128)} %pad_add_fusion.place_ref, bf16[680,1024]{1,0:T(8,128)(2,1)} %fusion.15.x_ref.own_ref, bf16[2,4,32,1536]{3,2,1,0:T(8,128)(2,1)} %pad_maximum_fusion.4.refs_0_, bf16[2,4,32,1536]{3,2,1,0:T(8,128)(2,1)} %pad_maximum_fusion.5.refs_1_, ...), custom_call_target="tpu_custom_call" | custom-call | flops 6417285120 | bytes 20938752 | tf_op jit(solution)/shard_map/gather_qkv/pallas_call | solution.py:258
  146.0 22.3 %attend.1 = (bf16[680,1024]{1,0:T(8,128)(2,1)S(1)}, f32[8,2,680]{2,1,0:T(2,128)S(1)}) custom-call(bf16[680,3072]{1,0:T(8,128)(2,1)} %get-tuple-element.78.q_ref.k_ref.v_ref, bf16[680,3072]{1,0:T(8,128)(2,1)} %get-tuple-element.78.q_ref.k_ref.v_ref, bf16[680,3072]{1,0:T(8,128)(2,1)} %get-tuple-element.78.q_ref.k_ref.v_ref, ...), custom_call_target="tpu_custom_call" | custom-call | flops 4734976000 | bytes 8355840 | tf_op jit(solution)/shard_map/attend/pallas_call | solution.py:114
  171.4 6.1 %gather_proj.1 = (bf16[1024,1024]{1,0:T(8,128)(2,1)}, f32[680,1024]{1,0:T(8,128)}) custom-call(s32[4]{0:T(128)} %pad_add_fusion.place_ref, bf16[680,1024]{1,0:T(8,128)(2,1)} %copy-done, bf16[2,4,32,2560]{3,2,1,0:T(8,128)(2,1)} %pad_maximum_fusion.refs_0_, bf16[2,4,32,2560]{3,2,1,0:T(8,128)(2,1)} %pad_maximum_fusion.1.refs_1_, ...), custom_call_target="tpu_custom_call" | custom-call | flops 2139095040 | bytes 6979584 | tf_op jit(solution)/shard_map/gather_proj/pallas_call | solution.py:258
  177.6 2.2 fusion.145
  183.0 14.7 %gather_fc1.1 = (bf16[1024,4096]{1,0:T(8,128)(2,1)}, f32[680,4096]{1,0:T(8,128)}, bf16[680,4096]{1,0:T(8,128)(2,1)}) custom-call(s32[4]{0:T(128)} %pad_add_fusion.place_ref, bf16[680,1024]{1,0:T(8,128)(2,1)} %add_convert_fusion.x_ref.own_ref, bf16[2,4,32,2560]{3,2,1,0:T(8,128)(2,1)} %pad_maximum_fusion.refs_0_, ...), custom_call_target="tpu_custom_call" | custom-call | flops 8556380160 | bytes 27918336 | tf_op jit(solution)/shard_map/gather_fc1/pallas_call | solution.py:258
  199.7 2.0 collective-permute-start.22
  201.7 5.5 collective-permute-done.24
  207.2 15.8 %collective-permute-done.23 = bf16[128,1024]{1,0:T(8,128)(2,1)S(1)} collective-permute-done((bf16[128,1024]{1,0:T(8,128)(2,1)S(1)}, bf16[128,1024]{1,0:T(8,128)(2,1)S(1)}, u32[]{:S(2)}, u32[]{:S(2)}) %collective-permute-start.23) | collective-permute-done | bytes 262176 | tf_op jit(solution)/shard_map/ppermute | solution.py:422
  223.5 2.1 collective-permute-start.26
  226.2 10.5 %collective-permute-done.25 = bf16[4,128,512]{2,1,0:T(8,128)(2,1)S(1)} collective-permute-done((bf16[4,128,512]{2,1,0:T(8,128)(2,1)S(1)}, bf16[4,128,512]{2,1,0:T(8,128)(2,1)S(1)}, u32[]{:S(2)}, u32[]{:S(2)}) %collective-permute-start.25) | collective-permute-done | bytes 524320 | tf_op jit(solution)/shard_map/ppermute | solution.py:416
  239.3 1.7 collective-permute-start.28
  241.1 1.7 fusion.23.grad_ref
  245.2 16.6 %collective-permute-done.27.refs_2_ = bf16[2,4,128,512]{3,2,1,0:T(8,128)(2,1)} collective-permute-done((bf16[2,4,128,512]{3,2,1,0:T(8,128)(2,1)}, bf16[2,4,128,512]{3,2,1,0:T(8,128)(2,1)}, u32[]{:S(2)}, u32[]{:S(2)}) %collective-permute-start.27) | collective-permute-done | bytes 1048608 | tf_op jit(solution)/shard_map/ppermute | solution.py:422
  263.1 15.4 %weight_grad.4 = (bf16[4,2,2,128,256]{4,3,2,1,0:T(8,128)(2,1)}, bf16[4,2,2,128,256]{4,3,2,1,0:T(8,128)(2,1)}, bf16[4,2,2,128,256]{4,3,2,1,0:T(8,128)(2,1)}, bf16[4,2,2,128,256]{4,3,2,1,0:T(8,128)(2,1)}) custom-call(s32[4]{0:T(128)} %pad_add_fusion.place_ref, bf16[680,4096]{1,0:T(8,128)(2,1)} %get-tuple-element.83.x_ref.own_ref, ...), custom_call_target="tpu_custom_call" | custom-call | flops 8556380160 | bytes 16728064 | tf_op jit(solution)/shard_map/weight_grad/pallas_call | solution.py:369
  278.5 2.3 copy.96
  282.8 12.8 %gather_fc2.1 = (bf16[4096,1024]{1,0:T(8,128)(2,1)}, f32[680,1024]{1,0:T(8,128)}) custom-call(s32[4]{0:T(128)} %pad_add_fusion.place_ref, bf16[680,4096]{1,0:T(8,128)(2,1)} %get-tuple-element.83.x_ref.own_ref, bf16[2,4,128,512]{3,2,1,0:T(8,128)(2,1)} %pad_maximum_fusion.2.refs_0_, bf16[2,4,128,512]{3,2,1,0:T(8,128)(2,1)} %pad_maximum_fusion.3.refs_1_, ...), custom_call_target="tpu_custom_call" | custom-call | flops 8556380160 | bytes 19562496 | tf_op jit(solution)/shard_map/gather_fc2/pallas_call | solution.py:258
  295.6 11.1 %collective-permute-done.65 = bf16[4,2,2,128,256]{4,3,2,0,1:T(8,128)(2,1)} collective-permute-done((bf16[4,2,2,128,256]{4,3,2,0,1:T(8,128)(2,1)}, bf16[4,2,2,128,256]{4,3,2,0,1:T(8,128)(2,1)}, u32[]{:S(2)}, u32[]{:S(2)}) %collective-permute-start.65) | collective-permute-done | bytes 1048608 | tf_op jit(solution)/shard_map/ppermute | solution.py:416
  306.7 1.8 convert_add_fusion.1
  314.0 18.0 %gelu_back.1 = (bf16[680,4096]{1,0:T(8,128)(2,1)}, bf16[680,2048]{1,0:T(8,128)(2,1)}) custom-call(s32[4]{0:T(128)S(1)} %copy-done.2, bf16[680,1024]{1,0:T(8,128)(2,1)S(1)} %fusion.23.grad_ref, bf16[4096,1024]{1,0:T(8,128)(2,1)} %get-tuple-element.90.weight_ref, f32[680,4096]{1,0:T(8,128)} %get-tuple-element.91.inner_ref), custom_call_target="tpu_custom_call" | custom-call | flops 8556380160 | bytes 30670848 | tf_op jit(solution)/shard_map/gelu_back/pallas_call | solution.py:304
  335.9 2.6 collective-permute-start.70
  338.5 1.9 collective-permute-start.69
  340.5 10.0 %fusion.150 = f32[680,1024]{1,0:T(8,128)} fusion(bf16[680,4096]{1,0:T(8,128)(2,1)S(1)} %copy-done.59, bf16[1024,4096]{1,0:T(8,128)(2,1)} %get-tuple-element.93), kind=kOutput, calls=%fused_computation.316 | convolution fusion | flops 5704253440 | bytes 16744448 | tf_op jit(solution)/shard_map/dot_general | solution.py:66
  350.6 11.2 %collective-permute-done.70 = bf16[2,128,512]{2,1,0:T(8,128)(2,1)S(1)} collective-permute-done((bf16[2,128,512]{2,1,0:T(8,128)(2,1)S(1)}, bf16[2,128,512]{2,1,0:T(8,128)(2,1)S(1)}, u32[]{:S(2)}, u32[]{:S(2)}) %collective-permute-start.70) | collective-permute-done | bytes 262176 | tf_op jit(solution)/shard_map/ppermute | solution.py:422
  362.0 12.6 %weight_grad.5 = (bf16[4,2,2,32,1024]{4,3,2,1,0:T(8,128)(2,1)}, bf16[4,2,2,32,1024]{4,3,2,1,0:T(8,128)(2,1)}, bf16[4,2,2,32,1024]{4,3,2,1,0:T(8,128)(2,1)}, bf16[4,2,2,32,1024]{4,3,2,1,0:T(8,128)(2,1)}) custom-call(s32[4]{0:T(128)} %pad_add_fusion.place_ref, bf16[680,1024]{1,0:T(8,128)(2,1)} %add_convert_fusion.x_ref.own_ref, ...), custom_call_target="tpu_custom_call" | custom-call | flops 8556380160 | bytes 12550144 | tf_op jit(solution)/shard_map/weight_grad/pallas_call | solution.py:369
  374.6 3.8 multiply_reduce_fusion
  386.4 2.8 convolution_convert_fusion.grad_ref
  390.1 6.0 %weight_grad.6 = (bf16[4,2,2,32,256]{4,3,2,1,0:T(8,128)(2,1)}, bf16[4,2,2,32,256]{4,3,2,1,0:T(8,128)(2,1)}, bf16[4,2,2,32,256]{4,3,2,1,0:T(8,128)(2,1)}, bf16[4,2,2,32,256]{4,3,2,1,0:T(8,128)(2,1)}) custom-call(s32[4]{0:T(128)} %pad_add_fusion.place_ref, bf16[680,1024]{1,0:T(8,128)(2,1)} %copy-done, bf16[680,1024]{1,0:T(8,128)(2,1)} %collective-permute-done.37.other_ref, ...), custom_call_target="tpu_custom_call" | custom-call | flops 2139095040 | bytes 5226496 | tf_op jit(solution)/shard_map/weight_grad/pallas_call | solution.py:369
  398.6 30.4 %attend_back.1.mine_ref = bf16[3,680,1024]{2,1,0:T(8,128)(2,1)} custom-call(bf16[680,3072]{1,0:T(8,128)(2,1)} %get-tuple-element.78.q_ref.k_ref.v_ref, bf16[680,3072]{1,0:T(8,128)(2,1)} %get-tuple-element.78.q_ref.k_ref.v_ref, bf16[680,3072]{1,0:T(8,128)(2,1)} %get-tuple-element.78.q_ref.k_ref.v_ref, bf16[680,1024]{1,0:T(8,128)(2,1)} %convolution_convert_fusion.grad_ref, ...), custom_call_target="tpu_custom_call" | custom-call | flops 9469952000 | bytes 11141120 | tf_op jit(solution)/shard_map/attend_back/pallas_call | solution.py:180
  429.0 1.9 constant_dynamic-slice_fusion
  431.4 1.8 collective-permute-start.50
  433.2 6.9 %collective-permute-done.51 = bf16[4,2,2,32,256]{4,3,2,1,0:T(8,128)(2,1)S(1)} collective-permute-done((bf16[4,2,2,32,256]{4,3,2,1,0:T(8,128)(2,1)S(1)}, bf16[4,2,2,32,256]{4,3,2,1,0:T(8,128)(2,1)S(1)}, u32[]{:S(2)}, u32[]{:S(2)}) %collective-permute-start.51) | collective-permute-done | bytes 262176 | tf_op jit(solution)/shard_map/ppermute | solution.py:422
  446.2 1.9 collective-permute-start.53
  448.3 1.7 collective-permute-done.55
  453.2 2.1 collective-permute-done.58
  455.5 6.0 %collective-permute-done.60 = bf16[4,2,32,1024]{3,2,1,0:T(8,128)(2,1)S(1)} collective-permute-done((bf16[4,2,32,1024]{3,2,1,0:T(8,128)(2,1)S(1)}, bf16[4,2,32,1024]{3,2,1,0:T(8,128)(2,1)S(1)}, u32[]{:S(2)}, u32[]{:S(2)}) %collective-permute-start.60) | collective-permute-done | bytes 524320 | tf_op jit(solution)/shard_map/ppermute | solution.py:416
  461.9 1.9 collective-permute-start.63
  466.6 4.2 collective-permute-done.63
  470.8 12.4 %collective-permute-done.62 = bf16[2,32,2048]{2,1,0:T(8,128)(2,1)S(1)} collective-permute-done((bf16[2,32,2048]{2,1,0:T(8,128)(2,1)S(1)}, bf16[2,32,2048]{2,1,0:T(8,128)(2,1)S(1)}, u32[]{:S(2)}, u32[]{:S(2)}) %collective-permute-start.62) | collective-permute-done | bytes 262176 | tf_op jit(solution)/shard_map/ppermute | solution.py:422
  487.4 11.2 %weight_grad.7 = (bf16[4,2,2,32,768]{4,3,2,1,0:T(8,128)(2,1)}, bf16[4,2,2,32,768]{4,3,2,1,0:T(8,128)(2,1)}, bf16[4,2,2,32,768]{4,3,2,1,0:T(8,128)(2,1)}, bf16[4,2,2,32,768]{4,3,2,1,0:T(8,128)(2,1)}) custom-call(s32[4]{0:T(128)} %pad_add_fusion.place_ref, bf16[680,1024]{1,0:T(8,128)(2,1)} %fusion.15.x_ref.own_ref, bf16[680,1024]{1,0:T(8,128)(2,1)} %copy-done.53, ...), custom_call_target="tpu_custom_call" | custom-call | flops 6417285120 | bytes 10108928 | tf_op jit(solution)/shard_map/weight_grad/pallas_call | solution.py:369
  499.7 2.6 slice_bitcast_fusion.2
  502.4 7.8 %fusion.131 = (bf16[1024]{0:T(1024)(128)(2,1)S(1)}, f32[680]{0:T(1024)S(1)}, f32[680,1024]{1,0:T(8,128)S(1)}) fusion(f32[1024]{0:T(1024)S(1)} %bitcast.320, f32[680]{0:T(1024)S(1)} %broadcast_multiply_fusion.1, bf16[1,680,1024]{2,1,0:T(8,128)(2,1)S(1)} %copy-done.7, bf16[1024,3072]{1,0:T(8,128)(2,1)} %get-tuple-element.103, ...), kind=kOutput, calls=%fused_computation.304 | convolution fusion | flops 4294899968 | bytes 14658880 | tf_op jit(solution)/shard_map/dot_general | solution.py:66
  513.8 3.9 fusion.24
  518.7 2.9 reduce.4
  522.7 3.9 all-to-all-start.3
  526.6 2.7 fusion.138
  529.3 10.0 %all-to-all-done.3 = bf16[32,2,3072]{2,1,0:T(2,128)(2,1)S(1)} async-done(((bf16[32,2,3072]{2,1,0:T(2,128)(2,1)}), bf16[32,2,3072]{2,1,0:T(2,128)(2,1)S(1)}, u32[]{:S(2)}, u32[]{:S(2)}) %all-to-all-start.3) | async-done | bytes 393248 | tf_op jit(solution)/shard_map/all_to_all | solution.py:637
  545.5 2.3 fusion.134
  547.9 5.3 collective-permute-done.42
  553.2 2.2 collective-permute-done.44
  558.4 4.5 collective-permute-done.47
  562.9 11.3 %collective-permute-done.46 = bf16[2,32,1536]{2,1,0:T(8,128)(2,1)S(1)} collective-permute-done((bf16[2,32,1536]{2,1,0:T(8,128)(2,1)S(1)}, bf16[2,32,1536]{2,1,0:T(8,128)(2,1)S(1)}, u32[]{:S(2)}, u32[]{:S(2)}) %collective-permute-start.46) | collective-permute-done | bytes 196640 | tf_op jit(solution)/shard_map/ppermute | solution.py:422
  (379 shorter events, 108.6 us)
Async XLA Ops:
  1.8 26.7 %collective-permute-start.2 = (bf16[32,3072]{1,0:T(8,128)(2,1)S(1)}, bf16[32,3072]{1,0:T(8,128)(2,1)S(1)}, u32[]{:S(2)}, u32[]{:S(2)}) collective-permute-start(bf16[32,3072]{1,0:T(8,128)(2,1)S(1)} %convert_element_type.320), channel_id=1, source_target_pairs={{0,24},{2,26},{4,28},{6,30},{8,0},{10,2},{12,4},{14,6},{16,8},{18,... | collective-permute-start | bytes 589832 | tf_op jit(solution)/shard_map/ppermute | solution.py:422
  6.9 21.7 %collective-permute-start.1 = (bf16[32,3072]{1,0:T(8,128)(2,1)S(1)}, bf16[32,3072]{1,0:T(8,128)(2,1)S(1)}, u32[]{:S(2)}, u32[]{:S(2)}) collective-permute-start(bf16[32,3072]{1,0:T(8,128)(2,1)S(1)} %convert_element_type.320), channel_id=1, source_target_pairs={{0,16},{2,18},{4,20},{6,22},{8,24},{10,26},{12,28},{14,30},{16,0},... | collective-permute-start | bytes 589832 | tf_op jit(solution)/shard_map/ppermute | solution.py:422
  6.9 21.7 %collective-permute-start = (bf16[32,3072]{1,0:T(8,128)(2,1)S(1)}, bf16[32,3072]{1,0:T(8,128)(2,1)S(1)}, u32[]{:S(2)}, u32[]{:S(2)}) collective-permute-start(bf16[32,3072]{1,0:T(8,128)(2,1)S(1)} %convert_element_type.320), channel_id=1, source_target_pairs={{0,8},{2,10},{4,12},{6,14},{8,16},{10,18},{12,20},{14,22},{16,24},... | collective-permute-start | bytes 589832 | tf_op jit(solution)/shard_map/ppermute | solution.py:422
  9.2 16.5 %all-to-all-start = ((s32[32,1,1]{2,1,0:T(1,128)}), s32[32,1,1]{2,1,0:T(1,128)S(1)}, u32[]{:S(2)}, u32[]{:S(2)}) async-start(s32[32,1,1]{2,1,0:T(1,128)} %broadcast_in_dim.71), calls=%async_computation | async-start | bytes 32768 | tf_op jit(solution)/shard_map/all_to_all | solution.py:496
  28.8 12.3 %collective-permute-start.5 = (bf16[32,5120]{1,0:T(8,128)(2,1)S(1)}, bf16[32,5120]{1,0:T(8,128)(2,1)}, u32[]{:S(2)}, u32[]{:S(2)}) collective-permute-start(bf16[32,5120]{1,0:T(8,128)(2,1)S(1)} %pad_maximum_fusion.16), channel_id=1, source_target_pairs={{0,24},{2,26},{4,28},{6,30},{8,0},{10,2},{12,4},{14,6},{16,8},{18,... | collective-permute-start | bytes 983048 | tf_op jit(solution)/shard_map/ppermute | solution.py:422
  32.6 31.6 %collective-permute-start.4 = (bf16[32,5120]{1,0:T(8,128)(2,1)S(1)}, bf16[32,5120]{1,0:T(8,128)(2,1)S(1)}, u32[]{:S(2)}, u32[]{:S(2)}) collective-permute-start(bf16[32,5120]{1,0:T(8,128)(2,1)S(1)} %pad_maximum_fusion.16), channel_id=1, source_target_pairs={{0,16},{2,18},{4,20},{6,22},{8,24},{10,26},{12,28},{14,30},{16,0},... | collective-permute-start | bytes 983048 | tf_op jit(solution)/shard_map/ppermute | solution.py:422
  32.6 34.7 %collective-permute-start.3 = (bf16[32,5120]{1,0:T(8,128)(2,1)S(1)}, bf16[32,5120]{1,0:T(8,128)(2,1)S(1)}, u32[]{:S(2)}, u32[]{:S(2)}) collective-permute-start(bf16[32,5120]{1,0:T(8,128)(2,1)S(1)} %pad_maximum_fusion.16), channel_id=1, source_target_pairs={{0,8},{2,10},{4,12},{6,14},{8,16},{10,18},{12,20},{14,22},{16,24},... | collective-permute-start | bytes 983048 | tf_op jit(solution)/shard_map/ppermute | solution.py:422
  34.8 32.8 %all-to-all-start.1 = ((f32[32,1,2048]{2,1,0:T(1,128)}), f32[32,1,2048]{2,1,0:T(1,128)S(1)}, u32[]{:S(2)}, u32[]{:S(2)}) async-start(f32[32,1,2048]{2,1,0:T(1,128)} %copy.85), calls=%async_computation.1 | async-start | bytes 524288 | tf_op jit(solution)/shard_map/all_to_all | solution.py:510
  37.9 26.4 %collective-permute-start.6 = (bf16[4,32,1536]{2,1,0:T(8,128)(2,1)S(1)}, bf16[4,32,1536]{2,1,0:T(8,128)(2,1)S(1)}, u32[]{:S(2)}, u32[]{:S(2)}) collective-permute-start(bf16[4,32,1536]{2,1,0:T(8,128)(2,1)S(1)} %get-tuple-element.74), channel_id=1, source_target_pairs={{0,1},{1,0},{2,3},{3,2},{4,5},{5,4},{6,7},{7,6},{8,9},{9,8},{10,11... | collective-permute-start | bytes 1179656 | tf_op jit(solution)/shard_map/ppermute | solution.py:416
  39.7 26.0 %collective-permute-start.8 = (bf16[4,32,1536]{2,1,0:T(8,128)(2,1)S(1)}, bf16[4,32,1536]{2,1,0:T(8,128)(2,1)S(1)}, u32[]{:S(2)}, u32[]{:S(2)}) collective-permute-start(bf16[4,32,1536]{2,1,0:T(8,128)(2,1)S(1)} %get-tuple-element.75), channel_id=1, source_target_pairs={{0,4},{2,6},{4,0},{6,2},{8,12},{10,14},{12,8},{14,10},{16,20},{18,... | collective-permute-start | bytes 1179656 | tf_op jit(solution)/shard_map/ppermute | solution.py:422
  65.2 18.1 %collective-permute-start.7 = (bf16[2,4,32,1536]{3,2,1,0:T(8,128)(2,1)}, bf16[2,4,32,1536]{3,2,1,0:T(8,128)(2,1)}, u32[]{:S(2)}, u32[]{:S(2)}) collective-permute-start(bf16[2,4,32,1536]{3,2,1,0:T(8,128)(2,1)} %pad_maximum_fusion.4.refs_0_), channel_id=1, source_target_pairs={{0,4},{2,6},{4,0},{6,2},{8,12},{10,14},{12,8},{14,10},{16,20},{18,... | collective-permute-start | bytes 2359304 | tf_op jit(solution)/shard_map/ppermute | solution.py:422
  66.7 17.9 %collective-permute-start.9 = (bf16[2,4,32,1536]{3,2,1,0:T(8,128)(2,1)}, bf16[2,4,32,1536]{3,2,1,0:T(8,128)(2,1)}, u32[]{:S(2)}, u32[]{:S(2)}) collective-permute-start(bf16[2,4,32,1536]{3,2,1,0:T(8,128)(2,1)} %pad_maximum_fusion.5.refs_1_), channel_id=1, source_target_pairs={{0,1},{1,0},{2,3},{3,2},{4,5},{5,4},{6,7},{7,6},{8,9},{9,8},{10,11... | collective-permute-start | bytes 2359304 | tf_op jit(solution)/shard_map/ppermute | solution.py:416
  84.6 13.9 %collective-permute-start.14 = (bf16[4,32,2560]{2,1,0:T(8,128)(2,1)S(1)}, bf16[4,32,2560]{2,1,0:T(8,128)(2,1)S(1)}, u32[]{:S(2)}, u32[]{:S(2)}) collective-permute-start(bf16[4,32,2560]{2,1,0:T(8,128)(2,1)S(1)} %pad_maximum_fusion.6), channel_id=1, source_target_pairs={{0,1},{1,0},{2,3},{3,2},{4,5},{5,4},{6,7},{7,6},{8,9},{9,8},{10,11... | collective-permute-start | bytes 1966088 | tf_op jit(solution)/shard_map/ppermute | solution.py:416
  86.9 15.9 %collective-permute-start.15 = (bf16[4,32,2560]{2,1,0:T(8,128)(2,1)S(1)}, bf16[4,32,2560]{2,1,0:T(8,128)(2,1)S(1)}, u32[]{:S(2)}, u32[]{:S(2)}) collective-permute-start(bf16[4,32,2560]{2,1,0:T(8,128)(2,1)S(1)} %pad_maximum_fusion.7), channel_id=1, source_target_pairs={{0,4},{2,6},{4,0},{6,2},{8,12},{10,14},{12,8},{14,10},{16,20},{18,... | collective-permute-start | bytes 1966088 | tf_op jit(solution)/shard_map/ppermute | solution.py:422
  88.8 18.3 %collective-permute-start.10 = (bf16[2,4,32,1536]{3,2,1,0:T(8,128)(2,1)}, bf16[2,4,32,1536]{3,2,1,0:T(8,128)(2,1)}, u32[]{:S(2)}, u32[]{:S(2)}) collective-permute-start(bf16[2,4,32,1536]{3,2,1,0:T(8,128)(2,1)} %pad_maximum_fusion.4.refs_0_), channel_id=1, source_target_pairs={{0,2},{2,0},{4,6},{6,4},{8,10},{10,8},{12,14},{14,12},{16,18},{18,... | collective-permute-start | bytes 2359304 | tf_op jit(solution)/shard_map/ppermute | solution.py:422
  99.7 34.3 %collective-permute-start.16 = (bf16[2,4,32,2560]{3,2,1,0:T(8,128)(2,1)}, bf16[2,4,32,2560]{3,2,1,0:T(8,128)(2,1)}, u32[]{:S(2)}, u32[]{:S(2)}) collective-permute-start(bf16[2,4,32,2560]{3,2,1,0:T(8,128)(2,1)} %pad_maximum_fusion.refs_0_), channel_id=1, source_target_pairs={{0,4},{2,6},{4,0},{6,2},{8,12},{10,14},{12,8},{14,10},{16,20},{18,... | collective-permute-start | bytes 3932168 | tf_op jit(solution)/shard_map/ppermute | solution.py:422
  104.0 30.7 %collective-permute-start.17 = (bf16[2,4,32,2560]{3,2,1,0:T(8,128)(2,1)}, bf16[2,4,32,2560]{3,2,1,0:T(8,128)(2,1)}, u32[]{:S(2)}, u32[]{:S(2)}) collective-permute-start(bf16[2,4,32,2560]{3,2,1,0:T(8,128)(2,1)} %pad_maximum_fusion.1.refs_1_), channel_id=1, source_target_pairs={{0,1},{1,0},{2,3},{3,2},{4,5},{5,4},{6,7},{7,6},{8,9},{9,8},{10,11... | collective-permute-start | bytes 3932168 | tf_op jit(solution)/shard_map/ppermute | solution.py:416
  107.2 29.2 %collective-permute-start.13 = (bf16[2,4,32,1536]{3,2,1,0:T(8,128)(2,1)}, bf16[2,4,32,1536]{3,2,1,0:T(8,128)(2,1)}, u32[]{:S(2)}, u32[]{:S(2)}) collective-permute-start(bf16[2,4,32,1536]{3,2,1,0:T(8,128)(2,1)} %collective-permute-done.9.refs_3_), channel_id=1, source_target_pairs={{0,2},{2,0},{4,6},{6,4},{8,10},{10,8},{12,14},{14,12},{16,18},{18,... | collective-permute-start | bytes 2359304 | tf_op jit(solution)/shard_map/ppermute | solution.py:422
  110.2 59.8 %all-to-all-start.2 = ((f32[32,1,4096]{2,1,0:T(1,128)}), f32[32,1,4096]{2,1,0:T(1,128)}, u32[]{:S(2)}, u32[]{:S(2)}) async-start(f32[32,1,4096]{2,1,0:T(1,128)} %copy.86), calls=%async_computation.2 | async-start | bytes 1048576 | tf_op jit(solution)/shard_map/all_to_all | solution.py:510
  114.1 57.3 %collective-permute-start.18 = (bf16[2,4,32,2560]{3,2,1,0:T(8,128)(2,1)}, bf16[2,4,32,2560]{3,2,1,0:T(8,128)(2,1)}, u32[]{:S(2)}, u32[]{:S(2)}) collective-permute-start(bf16[2,4,32,2560]{3,2,1,0:T(8,128)(2,1)} %pad_maximum_fusion.refs_0_), channel_id=1, source_target_pairs={{0,2},{2,0},{4,6},{6,4},{8,10},{10,8},{12,14},{14,12},{16,18},{18,... | collective-permute-start | bytes 3932168 | tf_op jit(solution)/shard_map/ppermute | solution.py:422
  114.4 57.0 %collective-permute-start.19 = (bf16[2,4,32,2560]{3,2,1,0:T(8,128)(2,1)}, bf16[2,4,32,2560]{3,2,1,0:T(8,128)(2,1)}, u32[]{:S(2)}, u32[]{:S(2)}) collective-permute-start(bf16[2,4,32,2560]{3,2,1,0:T(8,128)(2,1)} %pad_maximum_fusion.1.refs_1_), channel_id=1, source_target_pairs={{0,2},{2,0},{4,6},{6,4},{8,10},{10,8},{12,14},{14,12},{16,18},{18,... | collective-permute-start | bytes 3932168 | tf_op jit(solution)/shard_map/ppermute | solution.py:422
  133.9 37.5 %collective-permute-start.20 = (bf16[2,4,32,2560]{3,2,1,0:T(8,128)(2,1)}, bf16[2,4,32,2560]{3,2,1,0:T(8,128)(2,1)}, u32[]{:S(2)}, u32[]{:S(2)}) collective-permute-start(bf16[2,4,32,2560]{3,2,1,0:T(8,128)(2,1)} %collective-permute-done.16.refs_2_), channel_id=1, source_target_pairs={{0,2},{2,0},{4,6},{6,4},{8,10},{10,8},{12,14},{14,12},{16,18},{18,... | collective-permute-start | bytes 3932168 | tf_op jit(solution)/shard_map/ppermute | solution.py:422
  134.7 36.7 %collective-permute-start.21 = (bf16[2,4,32,2560]{3,2,1,0:T(8,128)(2,1)}, bf16[2,4,32,2560]{3,2,1,0:T(8,128)(2,1)}, u32[]{:S(2)}, u32[]{:S(2)}) collective-permute-start(bf16[2,4,32,2560]{3,2,1,0:T(8,128)(2,1)} %collective-permute-done.17.refs_3_), channel_id=1, source_target_pairs={{0,2},{2,0},{4,6},{6,4},{8,10},{10,8},{12,14},{14,12},{16,18},{18,... | collective-permute-start | bytes 3932168 | tf_op jit(solution)/shard_map/ppermute | solution.py:422
  197.7 65.4 %collective-permute-start.33 = (bf16[680,4096]{1,0:T(8,128)(2,1)}, bf16[680,4096]{1,0:T(8,128)(2,1)}, u32[]{:S(2)}, u32[]{:S(2)}) collective-permute-start(bf16[680,4096]{1,0:T(8,128)(2,1)} %get-tuple-element.83.x_ref.own_ref), channel_id=1, source_target_pairs={{0,2},{2,0},{4,6},{6,4},{8,10},{10,8},{12,14},{14,12},{16,18},{18,... | collective-permute-start | bytes 16711688 | tf_op jit(solution)/shard_map/ppermute | solution.py:422
  198.3 24.8 %collective-permute-start.23 = (bf16[128,1024]{1,0:T(8,128)(2,1)S(1)}, bf16[128,1024]{1,0:T(8,128)(2,1)S(1)}, u32[]{:S(2)}, u32[]{:S(2)}) collective-permute-start(bf16[128,1024]{1,0:T(8,128)(2,1)S(1)} %copy-done.28), channel_id=1, source_target_pairs={{0,16},{2,18},{4,20},{6,22},{8,24},{10,26},{12,28},{14,30},{16,0},... | collective-permute-start | bytes 786440 | tf_op jit(solution)/shard_map/ppermute | solution.py:422
  199.7 23.4 %collective-permute-start.22 = (bf16[128,1024]{1,0:T(8,128)(2,1)S(1)}, bf16[128,1024]{1,0:T(8,128)(2,1)S(1)}, u32[]{:S(2)}, u32[]{:S(2)}) collective-permute-start(bf16[128,1024]{1,0:T(8,128)(2,1)S(1)} %copy-done.28), channel_id=1, source_target_pairs={{0,8},{2,10},{4,12},{6,14},{8,16},{10,18},{12,20},{14,22},{16,24},... | collective-permute-start | bytes 786440 | tf_op jit(solution)/shard_map/ppermute | solution.py:422
  223.3 13.4 %collective-permute-start.25 = (bf16[4,128,512]{2,1,0:T(8,128)(2,1)S(1)}, bf16[4,128,512]{2,1,0:T(8,128)(2,1)S(1)}, u32[]{:S(2)}, u32[]{:S(2)}) collective-permute-start(bf16[4,128,512]{2,1,0:T(8,128)(2,1)S(1)} %pad_maximum_fusion.9), channel_id=1, source_target_pairs={{0,1},{1,0},{2,3},{3,2},{4,5},{5,4},{6,7},{7,6},{8,9},{9,8},{10,11... | collective-permute-start | bytes 1572872 | tf_op jit(solution)/shard_map/ppermute | solution.py:416
  223.5 14.8 %collective-permute-start.26 = (bf16[4,128,512]{2,1,0:T(8,128)(2,1)S(1)}, bf16[4,128,512]{2,1,0:T(8,128)(2,1)S(1)}, u32[]{:S(2)}, u32[]{:S(2)}) collective-permute-start(bf16[4,128,512]{2,1,0:T(8,128)(2,1)S(1)} %pad_maximum_fusion.10), channel_id=1, source_target_pairs={{0,4},{2,6},{4,0},{6,2},{8,12},{10,14},{12,8},{14,10},{16,20},{18,... | collective-permute-start | bytes 1572872 | tf_op jit(solution)/shard_map/ppermute | solution.py:422
  237.8 24.0 %collective-permute-start.27 = (bf16[2,4,128,512]{3,2,1,0:T(8,128)(2,1)}, bf16[2,4,128,512]{3,2,1,0:T(8,128)(2,1)}, u32[]{:S(2)}, u32[]{:S(2)}) collective-permute-start(bf16[2,4,128,512]{3,2,1,0:T(8,128)(2,1)} %pad_maximum_fusion.2.refs_0_), channel_id=1, source_target_pairs={{0,4},{2,6},{4,0},{6,2},{8,12},{10,14},{12,8},{14,10},{16,20},{18,... | collective-permute-start | bytes 3145736 | tf_op jit(solution)/shard_map/ppermute | solution.py:422
  239.3 23.8 %collective-permute-start.28 = (bf16[2,4,128,512]{3,2,1,0:T(8,128)(2,1)}, bf16[2,4,128,512]{3,2,1,0:T(8,128)(2,1)}, u32[]{:S(2)}, u32[]{:S(2)}) collective-permute-start(bf16[2,4,128,512]{3,2,1,0:T(8,128)(2,1)} %pad_maximum_fusion.3.refs_1_), channel_id=1, source_target_pairs={{0,1},{1,0},{2,3},{3,2},{4,5},{5,4},{6,7},{7,6},{8,9},{9,8},{10,11... | collective-permute-start | bytes 3145736 | tf_op jit(solution)/shard_map/ppermute | solution.py:416
  244.5 38.1 %collective-permute-start.29 = (bf16[2,4,128,512]{3,2,1,0:T(8,128)(2,1)}, bf16[2,4,128,512]{3,2,1,0:T(8,128)(2,1)}, u32[]{:S(2)}, u32[]{:S(2)}) collective-permute-start(bf16[2,4,128,512]{3,2,1,0:T(8,128)(2,1)} %pad_maximum_fusion.2.refs_0_), channel_id=1, source_target_pairs={{0,2},{2,0},{4,6},{6,4},{8,10},{10,8},{12,14},{14,12},{16,18},{18,... | collective-permute-start | bytes 3145736 | tf_op jit(solution)/shard_map/ppermute | solution.py:422
  245.1 37.7 %collective-permute-start.30 = (bf16[2,4,128,512]{3,2,1,0:T(8,128)(2,1)}, bf16[2,4,128,512]{3,2,1,0:T(8,128)(2,1)}, u32[]{:S(2)}, u32[]{:S(2)}) collective-permute-start(bf16[2,4,128,512]{3,2,1,0:T(8,128)(2,1)} %pad_maximum_fusion.3.refs_1_), channel_id=1, source_target_pairs={{0,2},{2,0},{4,6},{6,4},{8,10},{10,8},{12,14},{14,12},{16,18},{18,... | collective-permute-start | bytes 3145736 | tf_op jit(solution)/shard_map/ppermute | solution.py:422
  261.8 21.0 %collective-permute-start.31 = (bf16[2,4,128,512]{3,2,1,0:T(8,128)(2,1)}, bf16[2,4,128,512]{3,2,1,0:T(8,128)(2,1)}, u32[]{:S(2)}, u32[]{:S(2)}) collective-permute-start(bf16[2,4,128,512]{3,2,1,0:T(8,128)(2,1)} %collective-permute-done.27.refs_2_), channel_id=1, source_target_pairs={{0,2},{2,0},{4,6},{6,4},{8,10},{10,8},{12,14},{14,12},{16,18},{18,... | collective-permute-start | bytes 3145736 | tf_op jit(solution)/shard_map/ppermute | solution.py:422
  263.1 19.7 %collective-permute-start.32 = (bf16[2,4,128,512]{3,2,1,0:T(8,128)(2,1)}, bf16[2,4,128,512]{3,2,1,0:T(8,128)(2,1)}, u32[]{:S(2)}, u32[]{:S(2)}) collective-permute-start(bf16[2,4,128,512]{3,2,1,0:T(8,128)(2,1)} %collective-permute-done.28.refs_3_), channel_id=1, source_target_pairs={{0,2},{2,0},{4,6},{6,4},{8,10},{10,8},{12,14},{14,12},{16,18},{18,... | collective-permute-start | bytes 3145736 | tf_op jit(solution)/shard_map/ppermute | solution.py:422
  280.8 25.9 %collective-permute-start.65 = (bf16[4,2,2,128,256]{4,3,2,0,1:T(8,128)(2,1)}, bf16[4,2,2,128,256]{4,3,2,0,1:T(8,128)(2,1)}, u32[]{:S(2)}, u32[]{:S(2)}) collective-permute-start(bf16[4,2,2,128,256]{4,3,2,0,1:T(8,128)(2,1)} %copy.96), channel_id=1, source_target_pairs={{0,1},{1,0},{2,3},{3,2},{4,5},{5,4},{6,7},{7,6},{8,9},{9,8},{10,11... | collective-permute-start | bytes 3145736 | tf_op jit(solution)/shard_map/ppermute | solution.py:416
  282.5 28.5 %collective-permute-start.67 = (bf16[4,2,2,128,256]{4,3,2,1,0:T(8,128)(2,1)}, bf16[4,2,2,128,256]{4,3,2,1,0:T(8,128)(2,1)}, u32[]{:S(2)}, u32[]{:S(2)}) collective-permute-start(bf16[4,2,2,128,256]{4,3,2,1,0:T(8,128)(2,1)} %get-tuple-element.115), channel_id=1, source_target_pairs={{0,4},{2,6},{4,0},{6,2},{8,12},{10,14},{12,8},{14,10},{16,20},{18,... | collective-permute-start | bytes 3145736 | tf_op jit(solution)/shard_map/ppermute | solution.py:422
  309.5 23.0 %collective-permute-start.66 = (bf16[4,2,128,256]{3,2,1,0:T(8,128)(2,1)}, bf16[4,2,128,256]{3,2,1,0:T(8,128)(2,1)}, u32[]{:S(2)}, u32[]{:S(2)}) collective-permute-start(bf16[4,2,128,256]{3,2,1,0:T(8,128)(2,1)} %fusion.33), channel_id=1, source_target_pairs={{0,4},{2,6},{4,0},{6,2},{8,12},{10,14},{12,8},{14,10},{16,20},{18,... | collective-permute-start | bytes 1572872 | tf_op jit(solution)/shard_map/ppermute | solution.py:422
  313.5 20.6 %collective-permute-start.68 = (bf16[4,2,128,256]{3,2,1,0:T(8,128)(2,1)}, bf16[4,2,128,256]{3,2,1,0:T(8,128)(2,1)}, u32[]{:S(2)}, u32[]{:S(2)}) collective-permute-start(bf16[4,2,128,256]{3,2,1,0:T(8,128)(2,1)} %fusion.34), channel_id=1, source_target_pairs={{0,1},{1,0},{2,3},{3,2},{4,5},{5,4},{6,7},{7,6},{8,9},{9,8},{10,11... | collective-permute-start | bytes 1572872 | tf_op jit(solution)/shard_map/ppermute | solution.py:416
  331.9 30.0 %collective-permute-start.36 = (bf16[1,680,2048]{2,1,0:T(8,128)(2,1)}, bf16[1,680,2048]{2,1,0:T(8,128)(2,1)}, u32[]{:S(2)}, u32[]{:S(2)}) collective-permute-start(bf16[1,680,2048]{2,1,0:T(8,128)(2,1)} %bitcast.57), channel_id=1, source_target_pairs={{0,2},{2,0},{4,6},{6,4},{8,10},{10,8},{12,14},{14,12},{16,18},{18,... | collective-permute-start | bytes 8355848 | tf_op jit(solution)/shard_map/ppermute | solution.py:422
  332.0 29.9 %collective-permute-start.35 = (bf16[680,1024]{1,0:T(8,128)(2,1)}, bf16[680,1024]{1,0:T(8,128)(2,1)}, u32[]{:S(2)}, u32[]{:S(2)}) collective-permute-start(bf16[680,1024]{1,0:T(8,128)(2,1)} %add_convert_fusion.x_ref.own_ref), channel_id=1, source_target_pairs={{0,2},{2,0},{4,6},{6,4},{8,10},{10,8},{12,14},{14,12},{16,18},{18,... | collective-permute-start | bytes 4177928 | tf_op jit(solution)/shard_map/ppermute | solution.py:422
  335.9 14.7 %collective-permute-start.71 = (bf16[2,128,512]{2,1,0:T(8,128)(2,1)S(1)}, bf16[2,128,512]{2,1,0:T(8,128)(2,1)S(1)}, u32[]{:S(2)}, u32[]{:S(2)}) collective-permute-start(bf16[2,128,512]{2,1,0:T(8,128)(2,1)S(1)} %get-tuple-element.160), channel_id=1, source_target_pairs={{0,24},{2,26},{4,28},{6,30},{8,0},{10,2},{12,4},{14,6},{16,8},{18,... | collective-permute-start | bytes 786440 | tf_op jit(solution)/shard_map/ppermute | solution.py:422
  335.9 25.8 %collective-permute-start.70 = (bf16[2,128,512]{2,1,0:T(8,128)(2,1)S(1)}, bf16[2,128,512]{2,1,0:T(8,128)(2,1)S(1)}, u32[]{:S(2)}, u32[]{:S(2)}) collective-permute-start(bf16[2,128,512]{2,1,0:T(8,128)(2,1)S(1)} %get-tuple-element.159), channel_id=1, source_target_pairs={{0,16},{2,18},{4,20},{6,22},{8,24},{10,26},{12,28},{14,30},{16,0},... | collective-permute-start | bytes 786440 | tf_op jit(solution)/shard_map/ppermute | solution.py:422
  338.5 23.2 %collective-permute-start.69 = (bf16[2,128,512]{2,1,0:T(8,128)(2,1)S(1)}, bf16[2,128,512]{2,1,0:T(8,128)(2,1)S(1)}, u32[]{:S(2)}, u32[]{:S(2)}) collective-permute-start(bf16[2,128,512]{2,1,0:T(8,128)(2,1)S(1)} %get-tuple-element.158), channel_id=1, source_target_pairs={{0,8},{2,10},{4,12},{6,14},{8,16},{10,18},{12,20},{14,22},{16,24},... | collective-permute-start | bytes 786440 | tf_op jit(solution)/shard_map/ppermute | solution.py:422
  350.5 38.6 %collective-permute-start.37 = (bf16[680,1024]{1,0:T(8,128)(2,1)S(1)}, bf16[680,1024]{1,0:T(8,128)(2,1)}, u32[]{:S(2)}, u32[]{:S(2)}) collective-permute-start(bf16[680,1024]{1,0:T(8,128)(2,1)S(1)} %copy-done.1), channel_id=1, source_target_pairs={{0,2},{2,0},{4,6},{6,4},{8,10},{10,8},{12,14},{14,12},{16,18},{18,... | collective-permute-start | bytes 4177928 | tf_op jit(solution)/shard_map/ppermute | solution.py:422
  361.9 20.1 %collective-permute-start.72 = (f32[128,512]{1,0:T(8,128)S(1)}, f32[128,512]{1,0:T(8,128)S(1)}, u32[]{:S(2)}, u32[]{:S(2)}) collective-permute-start(f32[128,512]{1,0:T(8,128)S(1)} %dynamic-slice_bitcast_fusion.2), channel_id=1, source_target_pairs={{0,2},{2,0},{4,6},{6,4},{8,10},{10,8},{12,14},{14,12},{16,18},{18,... | collective-permute-start | bytes 786440 | tf_op jit(solution)/shard_map/ppermute | solution.py:422
  384.2 56.7 %collective-permute-start.57 = (bf16[4,2,2,32,1024]{4,3,2,0,1:T(8,128)(2,1)}, bf16[4,2,2,32,1024]{4,3,2,0,1:T(8,128)(2,1)}, u32[]{:S(2)}, u32[]{:S(2)}) collective-permute-start(bf16[4,2,2,32,1024]{4,3,2,0,1:T(8,128)(2,1)} %copy.93), channel_id=1, source_target_pairs={{0,1},{1,0},{2,3},{3,2},{4,5},{5,4},{6,7},{7,6},{8,9},{9,8},{10,11... | collective-permute-start | bytes 3145736 | tf_op jit(solution)/shard_map/ppermute | solution.py:416
  385.7 58.2 %collective-permute-start.59 = (bf16[4,2,2,32,1024]{4,3,2,1,0:T(8,128)(2,1)}, bf16[4,2,2,32,1024]{4,3,2,1,0:T(8,128)(2,1)}, u32[]{:S(2)}, u32[]{:S(2)}) collective-permute-start(bf16[4,2,2,32,1024]{4,3,2,1,0:T(8,128)(2,1)} %get-tuple-element.112), channel_id=1, source_target_pairs={{0,4},{2,6},{4,0},{6,2},{8,12},{10,14},{12,8},{14,10},{16,20},{18,... | collective-permute-start | bytes 3145736 | tf_op jit(solution)/shard_map/ppermute | solution.py:422
  397.1 34.3 %collective-permute-start.49 = (bf16[4,2,2,32,256]{4,3,2,0,1:T(8,128)(2,1)S(1)}, bf16[4,2,2,32,256]{4,3,2,0,1:T(8,128)(2,1)S(1)}, u32[]{:S(2)}, u32[]{:S(2)}) collective-permute-start(bf16[4,2,2,32,256]{4,3,2,0,1:T(8,128)(2,1)S(1)} %copy.90), channel_id=1, source_target_pairs={{0,1},{1,0},{2,3},{3,2},{4,5},{5,4},{6,7},{7,6},{8,9},{9,8},{10,11... | collective-permute-start | bytes 786440 | tf_op jit(solution)/shard_map/ppermute | solution.py:416
  430.8 56.5 %collective-permute-start.40 = (bf16[3,680,512]{2,1,0:T(8,128)(2,1)S(1)}, bf16[3,680,512]{2,1,0:T(8,128)(2,1)}, u32[]{:S(2)}, u32[]{:S(2)}) collective-permute-start(bf16[3,680,512]{2,1,0:T(8,128)(2,1)S(1)} %constant_dynamic-slice_fusion), channel_id=1, source_target_pairs={{0,2},{2,0},{4,6},{6,4},{8,10},{10,8},{12,14},{14,12},{16,18},{18,... | collective-permute-start | bytes 6266888 | tf_op jit(solution)/shard_map/ppermute | solution.py:422
  430.9 9.2 %collective-permute-start.51 = (bf16[4,2,2,32,256]{4,3,2,1,0:T(8,128)(2,1)S(1)}, bf16[4,2,2,32,256]{4,3,2,1,0:T(8,128)(2,1)S(1)}, u32[]{:S(2)}, u32[]{:S(2)}) collective-permute-start(bf16[4,2,2,32,256]{4,3,2,1,0:T(8,128)(2,1)S(1)} %copy-done.56), channel_id=1, source_target_pairs={{0,4},{2,6},{4,0},{6,2},{8,12},{10,14},{12,8},{14,10},{16,20},{18,... | collective-permute-start | bytes 786440 | tf_op jit(solution)/shard_map/ppermute | solution.py:422
  431.4 14.1 %collective-permute-start.50 = (bf16[4,2,32,256]{3,2,1,0:T(8,128)(2,1)S(1)}, bf16[4,2,32,256]{3,2,1,0:T(8,128)(2,1)S(1)}, u32[]{:S(2)}, u32[]{:S(2)}) collective-permute-start(bf16[4,2,32,256]{3,2,1,0:T(8,128)(2,1)S(1)} %fusion.92), channel_id=1, source_target_pairs={{0,4},{2,6},{4,0},{6,2},{8,12},{10,14},{12,8},{14,10},{16,20},{18,... | collective-permute-start | bytes 393224 | tf_op jit(solution)/shard_map/ppermute | solution.py:422
  442.6 12.8 %collective-permute-start.58 = (bf16[4,2,32,1024]{3,2,1,0:T(8,128)(2,1)S(1)}, bf16[4,2,32,1024]{3,2,1,0:T(8,128)(2,1)S(1)}, u32[]{:S(2)}, u32[]{:S(2)}) collective-permute-start(bf16[4,2,32,1024]{3,2,1,0:T(8,128)(2,1)S(1)} %fusion.31), channel_id=1, source_target_pairs={{0,4},{2,6},{4,0},{6,2},{8,12},{10,14},{12,8},{14,10},{16,20},{18,... | collective-permute-start | bytes 1572872 | tf_op jit(solution)/shard_map/ppermute | solution.py:422
  450.0 11.6 %collective-permute-start.60 = (bf16[4,2,32,1024]{3,2,1,0:T(8,128)(2,1)S(1)}, bf16[4,2,32,1024]{3,2,1,0:T(8,128)(2,1)S(1)}, u32[]{:S(2)}, u32[]{:S(2)}) collective-permute-start(bf16[4,2,32,1024]{3,2,1,0:T(8,128)(2,1)S(1)} %fusion.32), channel_id=1, source_target_pairs={{0,1},{1,0},{2,3},{3,2},{4,5},{5,4},{6,7},{7,6},{8,9},{9,8},{10,11... | collective-permute-start | bytes 1572872 | tf_op jit(solution)/shard_map/ppermute | solution.py:416
  453.1 13.2 %collective-permute-start.56 = (f32[32,512]{1,0:T(8,128)S(1)}, f32[32,512]{1,0:T(8,128)S(1)}, u32[]{:S(2)}, u32[]{:S(2)}) collective-permute-start(f32[32,512]{1,0:T(8,128)S(1)} %dynamic-slice_bitcast_fusion.5), channel_id=1, source_target_pairs={{0,2},{2,0},{4,6},{6,4},{8,10},{10,8},{12,14},{14,12},{16,18},{18,... | collective-permute-start | bytes 196616 | tf_op jit(solution)/shard_map/ppermute | solution.py:422
  463.7 19.4 %collective-permute-start.62 = (bf16[2,32,2048]{2,1,0:T(8,128)(2,1)S(1)}, bf16[2,32,2048]{2,1,0:T(8,128)(2,1)S(1)}, u32[]{:S(2)}, u32[]{:S(2)}) collective-permute-start(bf16[2,32,2048]{2,1,0:T(8,128)(2,1)S(1)} %get-tuple-element.162), channel_id=1, source_target_pairs={{0,16},{2,18},{4,20},{6,22},{8,24},{10,26},{12,28},{14,30},{16,0},... | collective-permute-start | bytes 786440 | tf_op jit(solution)/shard_map/ppermute | solution.py:422
  463.7 19.4 %collective-permute-start.61 = (bf16[2,32,2048]{2,1,0:T(8,128)(2,1)S(1)}, bf16[2,32,2048]{2,1,0:T(8,128)(2,1)S(1)}, u32[]{:S(2)}, u32[]{:S(2)}) collective-permute-start(bf16[2,32,2048]{2,1,0:T(8,128)(2,1)S(1)} %get-tuple-element.161), channel_id=1, source_target_pairs={{0,8},{2,10},{4,12},{6,14},{8,16},{10,18},{12,20},{14,22},{16,24},... | collective-permute-start | bytes 786440 | tf_op jit(solution)/shard_map/ppermute | solution.py:422
  466.3 19.9 %collective-permute-start.39 = (bf16[680,1024]{1,0:T(8,128)(2,1)S(1)}, bf16[680,1024]{1,0:T(8,128)(2,1)S(1)}, u32[]{:S(2)}, u32[]{:S(2)}) collective-permute-start(bf16[680,1024]{1,0:T(8,128)(2,1)S(1)} %copy-done.27), channel_id=1, source_target_pairs={{0,2},{2,0},{4,6},{6,4},{8,10},{10,8},{12,14},{14,12},{16,18},{18,... | collective-permute-start | bytes 4177928 | tf_op jit(solution)/shard_map/ppermute | solution.py:422
  511.6 28.1 %collective-permute-start.41 = (bf16[4,2,2,32,768]{4,3,2,0,1:T(8,128)(2,1)S(1)}, bf16[4,2,2,32,768]{4,3,2,0,1:T(8,128)(2,1)}, u32[]{:S(2)}, u32[]{:S(2)}) collective-permute-start(bf16[4,2,2,32,768]{4,3,2,0,1:T(8,128)(2,1)S(1)} %copy.88), channel_id=1, source_target_pairs={{0,1},{1,0},{2,3},{3,2},{4,5},{5,4},{6,7},{7,6},{8,9},{9,8},{10,11... | collective-permute-start | bytes 2359304 | tf_op jit(solution)/shard_map/ppermute | solution.py:416
  512.2 30.2 %collective-permute-start.43 = (bf16[4,2,2,32,768]{4,3,2,1,0:T(8,128)(2,1)}, bf16[4,2,2,32,768]{4,3,2,1,0:T(8,128)(2,1)}, u32[]{:S(2)}, u32[]{:S(2)}) collective-permute-start(bf16[4,2,2,32,768]{4,3,2,1,0:T(8,128)(2,1)} %get-tuple-element.106), channel_id=1, source_target_pairs={{0,4},{2,6},{4,0},{6,2},{8,12},{10,14},{12,8},{14,10},{16,20},{18,... | collective-permute-start | bytes 2359304 | tf_op jit(solution)/shard_map/ppermute | solution.py:422
  522.7 16.6 %all-to-all-start.3 = ((bf16[32,2,3072]{2,1,0:T(2,128)(2,1)}), bf16[32,2,3072]{2,1,0:T(2,128)(2,1)S(1)}, u32[]{:S(2)}, u32[]{:S(2)}) async-start(bf16[32,2,3072]{2,1,0:T(2,128)(2,1)} %reshape.282), calls=%async_computation.3 | async-start | bytes 786432 | tf_op jit(solution)/shard_map/all_to_all | solution.py:637
  541.4 11.8 %collective-permute-start.42 = (bf16[4,2,32,768]{3,2,1,0:T(8,128)(2,1)S(1)}, bf16[4,2,32,768]{3,2,1,0:T(8,128)(2,1)S(1)}, u32[]{:S(2)}, u32[]{:S(2)}) collective-permute-start(bf16[4,2,32,768]{3,2,1,0:T(8,128)(2,1)S(1)} %fusion.58), channel_id=1, source_target_pairs={{0,4},{2,6},{4,0},{6,2},{8,12},{10,14},{12,8},{14,10},{16,20},{18,... | collective-permute-start | bytes 1179656 | tf_op jit(solution)/shard_map/ppermute | solution.py:422
  544.0 11.4 %collective-permute-start.44 = (bf16[4,2,32,768]{3,2,1,0:T(8,128)(2,1)S(1)}, bf16[4,2,32,768]{3,2,1,0:T(8,128)(2,1)S(1)}, u32[]{:S(2)}, u32[]{:S(2)}) collective-permute-start(bf16[4,2,32,768]{3,2,1,0:T(8,128)(2,1)S(1)} %fusion.59), channel_id=1, source_target_pairs={{0,1},{1,0},{2,3},{3,2},{4,5},{5,4},{6,7},{7,6},{8,9},{9,8},{10,11... | collective-permute-start | bytes 1179656 | tf_op jit(solution)/shard_map/ppermute | solution.py:416
  557.1 17.0 %collective-permute-start.46 = (bf16[2,32,1536]{2,1,0:T(8,128)(2,1)S(1)}, bf16[2,32,1536]{2,1,0:T(8,128)(2,1)S(1)}, u32[]{:S(2)}, u32[]{:S(2)}) collective-permute-start(bf16[2,32,1536]{2,1,0:T(8,128)(2,1)S(1)} %get-tuple-element.165), channel_id=1, source_target_pairs={{0,16},{2,18},{4,20},{6,22},{8,24},{10,26},{12,28},{14,30},{16,0},... | collective-permute-start | bytes 589832 | tf_op jit(solution)/shard_map/ppermute | solution.py:422
  557.6 16.6 %collective-permute-start.45 = (bf16[2,32,1536]{2,1,0:T(8,128)(2,1)S(1)}, bf16[2,32,1536]{2,1,0:T(8,128)(2,1)S(1)}, u32[]{:S(2)}, u32[]{:S(2)}) collective-permute-start(bf16[2,32,1536]{2,1,0:T(8,128)(2,1)S(1)} %get-tuple-element.164), channel_id=1, source_target_pairs={{0,8},{2,10},{4,12},{6,14},{8,16},{10,18},{12,20},{14,22},{16,24},... | collective-permute-start | bytes 589832 | tf_op jit(solution)/shard_map/ppermute | solution.py:422
  (74 other events, 602.2 us)
